TPU v7x, 32 devices: a whole 2x2x4 slice. The times are simulated.
32 devices in a mesh: seq: 4 (over x, core), dp: 8 (over z, y).
Axes of the slice: x: 2, y: 2, z: 4, core: 2. Of those that a mesh axis runs over, the one named last changes fastest.
Arguments:
- tokens: bfloat16 [8, 1280, 960], P('dp', 'seq'), may hold values from -6 to 6
- seg_ids: int32 [8, 1280], P('dp', 'seq'), may hold values from 0 to 4, as said below
- positions: int32 [8, 1280], P('dp', 'seq'), may hold values from 0 to 1279, as said below
- attn_gain: float32 [960], replicated, may hold values from 0.25 to 1.75
- w_query: bfloat16 [960, 960], replicated, may hold values from -0.1875 to 0.1875
- w_key: bfloat16 [960, 320], replicated, may hold values from -0.1875 to 0.1875
- w_value: bfloat16 [960, 320], replicated, may hold values from -0.1875 to 0.1875
- w_out: bfloat16 [960, 960], replicated, may hold values from -0.5 to 0.5
- ffn_gain: float32 [960], replicated, may hold values from 0.25 to 1.75
- w_gate: bfloat16 [960, 2560], P(None, 'seq'), may hold values from -0.1875 to 0.1875
- w_up: bfloat16 [960, 2560], P(None, 'seq'), may hold values from -0.1875 to 0.1875
- w_down: bfloat16 [2560, 960], P('seq'), may hold values from -0.125 to 0.125
- cotangent: bfloat16 [8, 1280, 960], P('dp', 'seq'), may hold values from -6 to 6
Outputs:
- output: bfloat16 [8, 1280, 960], P('dp', 'seq')
- input_grad: float32 [8, 1280, 960], P('dp', 'seq')
- attn_gain_grad: float32 [960], P('dp')
- w_query_grad: float32 [960, 960], P('dp')
- w_key_grad: float32 [960, 320], P('dp')
- w_value_grad: float32 [960, 320], P('dp')
- w_out_grad: float32 [960, 960], P('dp')
- ffn_gain_grad: float32 [960], P('dp')
- w_gate_grad: float32 [960, 2560], P('dp', 'seq')
- w_up_grad: float32 [960, 2560], P('dp', 'seq')
- w_down_grad: float32 [2560, 960], P('seq', 'dp')
Inputs may be any that keep to these rules, and one draw needn't show every extreme that they name: `seg_ids`: within a row the ids start at 0 and never fall. `positions`: A token's position counts the tokens before it in its document (0 at a document's first token).
All inputs are finite; a program needn't handle non-finite values.
Results may differ from a plain program's by a relative error of at most 0.025.
Values may be sent and summed in bfloat16 or wider, within the bound.
A program may use at most 256 MiB of HBM per device.

v0:
```python
import jax
import jax.numpy as jnp
from jax import lax
from jax.sharding import PartitionSpec as P

HEADS = 15
KV_HEADS = 5
HEAD_DIM = 64


EPSILON = 1e-05
THETA = 10000.0
MASKED = -1e30


def rope_tables(positions):
    half_dim = HEAD_DIM // 2
    frequency = THETA ** (-(jnp.arange(half_dim, dtype=jnp.float32) * 2.0 / HEAD_DIM))
    angles = positions.astype(jnp.float32)[..., None] * frequency
    return (jnp.cos(angles), jnp.sin(angles))


def rotate(values, cos_table, sin_table):
    half_dim = values.shape[-1] // 2
    first_half = values[..., :half_dim]
    second_half = values[..., half_dim:]
    cos_head = cos_table[..., None, :]
    sin_head = sin_table[..., None, :]
    return jnp.concatenate(
        [
            first_half * cos_head - second_half * sin_head,
            second_half * cos_head + first_half * sin_head,
        ],
        axis=-1,
    )


def norm_forward(residual, gain_vec):
    inverse = lax.rsqrt(jnp.mean(residual * residual, axis=-1, keepdims=True) + EPSILON)
    return ((residual * inverse * gain_vec).astype(jnp.bfloat16), inverse)


def norm_backward(residual, inverse, gain_vec, upstream):
    weighted = upstream * gain_vec
    inner_mean = jnp.mean(weighted * residual, axis=-1, keepdims=True)
    residual_grad = inverse * weighted - residual * (inverse * inverse * inverse) * inner_mean
    gain_grad = jnp.sum(upstream * residual * inverse, axis=(0, 1))
    return (residual_grad, gain_grad)


def masked_scores(queries, keys_all, allowed):
    raw_scores = jnp.einsum("qkgd,tkd->kgqt", queries, keys_all, preferred_element_type=jnp.float32)
    return jnp.where(allowed[None, None], raw_scores * HEAD_DIM ** (-0.5), MASKED)


def row_attend(operands):
    queries, keys_all, values_all, allowed = operands
    scores = masked_scores(queries, keys_all, allowed)
    row_max = jnp.max(scores, axis=-1, keepdims=True)
    shifted = jnp.exp(scores - row_max)
    row_total = jnp.sum(shifted, axis=-1, keepdims=True)
    probs_low = (shifted / row_total).astype(jnp.bfloat16)
    mixed_heads = jnp.einsum(
        "kgqt,tkd->qkgd", probs_low, values_all, preferred_element_type=jnp.float32
    )
    return (mixed_heads, row_max + jnp.log(row_total))


def row_backward(operands):
    queries, keys_all, values_all, allowed, log_total, mixed_grad = operands
    scores = masked_scores(queries, keys_all, allowed)
    weights_soft = jnp.exp(scores - log_total)
    probs_grad = jnp.einsum(
        "qkgd,tkd->kgqt", mixed_grad, values_all, preferred_element_type=jnp.float32
    )
    row_delta = jnp.sum(probs_grad * weights_soft, axis=-1, keepdims=True)
    score_grad = (weights_soft * (probs_grad - row_delta)).astype(jnp.bfloat16)
    score_scale = HEAD_DIM ** (-0.5)
    query_grad = (
        jnp.einsum("kgqt,tkd->qkgd", score_grad, keys_all, preferred_element_type=jnp.float32)
        * score_scale
    )
    key_grad = (
        jnp.einsum("kgqt,qkgd->tkd", score_grad, queries, preferred_element_type=jnp.float32)
        * score_scale
    )
    value_grad = jnp.einsum(
        "kgqt,qkgd->tkd",
        weights_soft.astype(jnp.bfloat16),
        mixed_grad,
        preferred_element_type=jnp.float32,
    )
    return (query_grad, key_grad, value_grad)


def on_device(
    tokens,
    seg_ids,
    positions,
    attn_gain,
    w_query,
    w_key,
    w_value,
    w_out,
    ffn_gain,
    w_gate,
    w_up,
    w_down,
    cotangent,
):
    row_count, shard_len, model_width = tokens.shape
    row_len = shard_len * lax.axis_size("seq")
    groups = HEADS // KV_HEADS
    kv_width = KV_HEADS * HEAD_DIM
    doc_all = lax.all_gather(seg_ids, "seq", axis=1, tiled=True)
    query_place = lax.axis_index("seq") * shard_len + jnp.arange(shard_len, dtype=jnp.int32)
    key_place = jnp.arange(row_len, dtype=jnp.int32)
    allowed = (seg_ids[:, :, None] == doc_all[:, None, :]) & (
        key_place[None, None, :] <= query_place[None, :, None]
    )
    cos_table, sin_table = rope_tables(positions)
    gate_mat, up_mat, down_mat = (
        lax.all_gather(w_gate, "seq", axis=1, tiled=True),
        lax.all_gather(w_up, "seq", axis=1, tiled=True),
        lax.all_gather(w_down, "seq", axis=0, tiled=True),
    )
    residual = tokens.astype(jnp.float32)
    kept_runs = []
    for repeat in range(2):
        normed, attn_inverse = norm_forward(residual, attn_gain)
        query_pre = jnp.einsum("rcd,de->rce", normed, w_query, preferred_element_type=jnp.float32)
        key_pre = jnp.einsum("rcd,de->rce", normed, w_key, preferred_element_type=jnp.float32)
        value_pre = jnp.einsum("rcd,de->rce", normed, w_value, preferred_element_type=jnp.float32)
        queries = rotate(
            query_pre.reshape(row_count, shard_len, HEADS, HEAD_DIM), cos_table, sin_table
        ).astype(jnp.bfloat16)
        keys_local = rotate(
            key_pre.reshape(row_count, shard_len, KV_HEADS, HEAD_DIM), cos_table, sin_table
        ).astype(jnp.bfloat16)
        joined = jnp.concatenate(
            [keys_local.reshape(row_count, shard_len, kv_width), value_pre.astype(jnp.bfloat16)],
            axis=-1,
        )
        joined_all = lax.all_gather(joined, "seq", axis=1, tiled=True)
        keys_all = joined_all[..., :kv_width].reshape(row_count, row_len, KV_HEADS, HEAD_DIM)
        values_all = joined_all[..., kv_width:].reshape(row_count, row_len, KV_HEADS, HEAD_DIM)
        grouped = queries.reshape(row_count, shard_len, KV_HEADS, groups, HEAD_DIM)
        mixed_heads, log_total = lax.map(row_attend, (grouped, keys_all, values_all, allowed))
        mixed_low = mixed_heads.reshape(row_count, shard_len, HEADS * HEAD_DIM).astype(jnp.bfloat16)
        after_attn = residual + jnp.einsum(
            "rce,ed->rcd", mixed_low, w_out, preferred_element_type=jnp.float32
        )
        normed_two, ffn_inverse = norm_forward(after_attn, ffn_gain)
        gate_pre = jnp.einsum(
            "rtd,df->rtf", normed_two, gate_mat, preferred_element_type=jnp.float32
        )
        up_pre = jnp.einsum("rtd,df->rtf", normed_two, up_mat, preferred_element_type=jnp.float32)
        ffn_hidden = (jax.nn.silu(gate_pre) * up_pre).astype(jnp.bfloat16)
        partial_sum = jnp.einsum(
            "rtf,fd->rtd", ffn_hidden, down_mat, preferred_element_type=jnp.float32
        )
        normed_rows, gate_pre, up_pre, ffn_out = (normed_two, gate_pre, up_pre, partial_sum)
        kept_runs.append(
            (
                residual,
                normed,
                attn_inverse,
                grouped,
                keys_all,
                values_all,
                log_total,
                mixed_low,
                after_attn,
                ffn_inverse,
                normed_rows,
                gate_pre,
                up_pre,
            )
        )
        residual = after_attn + ffn_out
    output = residual.astype(jnp.bfloat16)
    attn_gain_grad = jnp.zeros(attn_gain.shape, jnp.float32)
    ffn_gain_grad = jnp.zeros(ffn_gain.shape, jnp.float32)
    w_query_grad = jnp.zeros(w_query.shape, jnp.float32)
    w_key_grad = jnp.zeros(w_key.shape, jnp.float32)
    w_value_grad = jnp.zeros(w_value.shape, jnp.float32)
    w_out_grad = jnp.zeros(w_out.shape, jnp.float32)
    w_gate_grad = jnp.zeros(gate_mat.shape, jnp.float32)
    w_up_grad = jnp.zeros(up_mat.shape, jnp.float32)
    w_down_grad = jnp.zeros(down_mat.shape, jnp.float32)
    upstream = cotangent.astype(jnp.float32)
    for repeat in (1, 0):
        (
            residual,
            normed,
            attn_inverse,
            grouped,
            keys_all,
            values_all,
            log_total,
            mixed_low,
            after_attn,
            ffn_inverse,
            normed_rows,
            gate_pre,
            up_pre,
        ) = kept_runs[repeat]
        ffn_grad = upstream.astype(jnp.bfloat16)
        sigmoid_gate = jax.nn.sigmoid(gate_pre)
        silu_gate = jax.nn.silu(gate_pre)
        hidden = (silu_gate * up_pre).astype(jnp.bfloat16)
        w_down_grad = w_down_grad + jnp.einsum(
            "rtf,rtd->fd", hidden, ffn_grad, preferred_element_type=jnp.float32
        )
        hidden_grad = jnp.einsum(
            "rtd,fd->rtf", ffn_grad, down_mat, preferred_element_type=jnp.float32
        )
        gate_grad = (
            hidden_grad * up_pre * sigmoid_gate * (1.0 + gate_pre * (1.0 - sigmoid_gate))
        ).astype(jnp.bfloat16)
        up_grad = (hidden_grad * silu_gate).astype(jnp.bfloat16)
        w_gate_grad = w_gate_grad + jnp.einsum(
            "rtd,rtf->df", normed_rows, gate_grad, preferred_element_type=jnp.float32
        )
        w_up_grad = w_up_grad + jnp.einsum(
            "rtd,rtf->df", normed_rows, up_grad, preferred_element_type=jnp.float32
        )
        normed_two_grad = jnp.einsum(
            "rtf,df->rtd", gate_grad, gate_mat, preferred_element_type=jnp.float32
        ) + jnp.einsum("rtf,df->rtd", up_grad, up_mat, preferred_element_type=jnp.float32)
        after_grad, gain_two = norm_backward(after_attn, ffn_inverse, ffn_gain, normed_two_grad)
        after_grad = after_grad + upstream
        ffn_gain_grad = ffn_gain_grad + gain_two
        attn_grad = after_grad.astype(jnp.bfloat16)
        w_out_grad = w_out_grad + jnp.einsum(
            "rce,rcd->ed", mixed_low, attn_grad, preferred_element_type=jnp.float32
        )
        mixed_grad = jnp.einsum(
            "rcd,ed->rce", attn_grad, w_out, preferred_element_type=jnp.float32
        ).astype(jnp.bfloat16)
        mixed_grad = mixed_grad.reshape(row_count, shard_len, KV_HEADS, groups, HEAD_DIM)
        query_grad, key_grad, value_grad = lax.map(
            row_backward, (grouped, keys_all, values_all, allowed, log_total, mixed_grad)
        )
        joined_grad = jnp.concatenate(
            [
                key_grad.reshape(row_count, row_len, kv_width),
                value_grad.reshape(row_count, row_len, kv_width),
            ],
            axis=-1,
        )
        local_grad = lax.psum_scatter(
            joined_grad.astype(jnp.bfloat16), "seq", scatter_dimension=1, tiled=True
        ).astype(jnp.float32)
        key_back = rotate(
            local_grad[..., :kv_width].reshape(row_count, shard_len, KV_HEADS, HEAD_DIM),
            cos_table,
            -sin_table,
        )
        key_back = key_back.reshape(row_count, shard_len, kv_width).astype(jnp.bfloat16)
        value_back = local_grad[..., kv_width:].astype(jnp.bfloat16)
        query_back = rotate(
            query_grad.reshape(row_count, shard_len, HEADS, HEAD_DIM), cos_table, -sin_table
        )
        query_back = query_back.reshape(row_count, shard_len, HEADS * HEAD_DIM).astype(jnp.bfloat16)
        w_query_grad = w_query_grad + jnp.einsum(
            "rcd,rce->de", normed, query_back, preferred_element_type=jnp.float32
        )
        w_key_grad = w_key_grad + jnp.einsum(
            "rcd,rce->de", normed, key_back, preferred_element_type=jnp.float32
        )
        w_value_grad = w_value_grad + jnp.einsum(
            "rcd,rce->de", normed, value_back, preferred_element_type=jnp.float32
        )
        normed_grad = jnp.einsum(
            "rce,de->rcd", query_back, w_query, preferred_element_type=jnp.float32
        )
        normed_grad = normed_grad + jnp.einsum(
            "rce,de->rcd", key_back, w_key, preferred_element_type=jnp.float32
        )
        normed_grad = normed_grad + jnp.einsum(
            "rce,de->rcd", value_back, w_value, preferred_element_type=jnp.float32
        )
        residual_grad, gain_one = norm_backward(residual, attn_inverse, attn_gain, normed_grad)
        attn_gain_grad = attn_gain_grad + gain_one
        upstream = residual_grad + after_grad
    w_gate_grad, w_up_grad, w_down_grad = (
        lax.psum_scatter(
            w_gate_grad.astype(jnp.bfloat16), "seq", scatter_dimension=1, tiled=True
        ).astype(jnp.float32),
        lax.psum_scatter(
            w_up_grad.astype(jnp.bfloat16), "seq", scatter_dimension=1, tiled=True
        ).astype(jnp.float32),
        lax.psum_scatter(
            w_down_grad.astype(jnp.bfloat16), "seq", scatter_dimension=0, tiled=True
        ).astype(jnp.float32),
    )
    shards = (
        lax.psum_scatter(attn_gain_grad, "dp", scatter_dimension=0, tiled=True),
        lax.psum_scatter(w_query_grad, "dp", scatter_dimension=0, tiled=True),
        lax.psum_scatter(w_key_grad, "dp", scatter_dimension=0, tiled=True),
        lax.psum_scatter(w_value_grad, "dp", scatter_dimension=0, tiled=True),
        lax.psum_scatter(w_out_grad, "dp", scatter_dimension=0, tiled=True),
        lax.psum_scatter(ffn_gain_grad, "dp", scatter_dimension=0, tiled=True),
        lax.psum_scatter(w_gate_grad, "dp", scatter_dimension=0, tiled=True),
        lax.psum_scatter(w_up_grad, "dp", scatter_dimension=0, tiled=True),
        lax.psum_scatter(w_down_grad, "dp", scatter_dimension=1, tiled=True),
    )
    attn_sums = (
        lax.psum(shards[0].astype(jnp.bfloat16), "seq").astype(jnp.float32),
        lax.psum(shards[1].astype(jnp.bfloat16), "seq").astype(jnp.float32),
        lax.psum(shards[2].astype(jnp.bfloat16), "seq").astype(jnp.float32),
        lax.psum(shards[3].astype(jnp.bfloat16), "seq").astype(jnp.float32),
        lax.psum(shards[4].astype(jnp.bfloat16), "seq").astype(jnp.float32),
        lax.psum(shards[5].astype(jnp.bfloat16), "seq").astype(jnp.float32),
    )
    return (
        output,
        upstream,
        attn_sums[0],
        attn_sums[1],
        attn_sums[2],
        attn_sums[3],
        attn_sums[4],
        attn_sums[5],
        shards[6],
        shards[7],
        shards[8],
    )


def solution(mesh):
    in_specs = (
        P("dp", "seq", None),
        P("dp", "seq"),
        P("dp", "seq"),
        P(),
        P(),
        P(),
        P(),
        P(),
        P(),
        P(None, "seq"),
        P(None, "seq"),
        P("seq", None),
        P("dp", "seq", None),
    )
    out_specs = (
        P("dp", "seq", None),
        P("dp", "seq", None),
        P("dp"),
        P("dp", None),
        P("dp", None),
        P("dp", None),
        P("dp", None),
        P("dp"),
        P("dp", "seq"),
        P("dp", "seq"),
        P("seq", "dp"),
    )
    return jax.shard_map(
        on_device, mesh=mesh, in_specs=in_specs, out_specs=out_specs, check_vma=False
    )
```

profile of v0, /device:TPU:0, one launch (start us, length us, event | category | flops | bytes accessed | tf_op | source)
XLA Modules:
  0.0 1120.8 jit_solution(3167693406144594181)
XLA Ops:
  45.4 13.7 %fusion.120 = (f32[5,3,320]{2,1,0:T(4,128)S(1)}, f32[5,3,320,1280]{3,2,1,0:T(8,128)}) fusion(bf16[1280,5,64,1]{0,2,3,1:T(8,128)(2,1)} %bitcast.365, bf16[320,5,3,32]{0,3,2,1:T(8,128)(2,1)} %bitcast.385, bf16[320,5,3,32]{0,3,2,1:T(8,128)(2,1)} %bitcast.383, pred[320,1280]{1,0:T(8,128)(4,1)S(1)} %fusion.36), kind=kOutput, calls=%fused_computation.230 | convolution fusion | flops 806088000 | bytes 26438400 | tf_op jit(solution)/shard_map/while/body/eval_jaxpr/qkgd,tkd->kgqt/dot_general | solution.py:52
  59.2 12.1 %fusion.6 = f32[5,3,320]{2,1,0:T(4,128)} fusion(f32[5,3,320,1280]{3,2,1,0:T(8,128)} %get-tuple-element.172, f32[5,3,320]{2,1,0:T(4,128)S(1)} %get-tuple-element.171), kind=kLoop, calls=%fused_computation.18 | loop fusion | flops 12283200 | bytes 24614400 | tf_op jit(solution)/shard_map/while/body/eval_jaxpr/reduce_sum | solution.py:61
  92.2 25.8 %all-gather.10.cloned.1.call-done = bf16[960,2560]{1,0:T(8,128)(2,1)} async-done(((bf16[960,640]{1,0:T(8,128)(2,1)}), bf16[960,2560]{1,0:T(8,128)(2,1)}) %all-gather.10.cloned.1.call-update) | async-done | bytes 4915216 | tf_op jit(solution)/shard_map/all_gather | solution.py:124
  125.8 32.2 %all-gather.12.cloned.1.call-done = bf16[2560,960]{0,1:T(8,128)(2,1)} async-done(((bf16[640,960]{0,1:T(8,128)(2,1)}), bf16[2560,960]{0,1:T(8,128)(2,1)}) %all-gather.12.cloned.1.call-update) | async-done | bytes 4915216 | tf_op jit(solution)/shard_map/all_gather | solution.py:125
  172.3 16.2 %all-gather.14.cloned.1.call-done = bf16[1,1280,640]{2,1,0:T(8,128)(2,1)} async-done(((bf16[1,320,640]{2,1,0:T(8,128)(2,1)}), bf16[1,1280,640]{2,1,0:T(8,128)(2,1)}) %all-gather.14.cloned.1.call-update) | async-done | bytes 1638416 | tf_op jit(solution)/shard_map/all_gather | solution.py:144
  194.8 12.4 %fusion.121 = (f32[5,3,320]{2,1,0:T(4,128)}, f32[5,3,320,1280]{3,2,1,0:T(8,128)}) fusion(bf16[1280,5,64,1]{0,2,3,1:T(8,128)(2,1)S(1)} %bitcast.367, bf16[320,5,3,32]{0,3,2,1:T(8,128)(2,1)} %bitcast.389, bf16[320,5,3,32]{0,3,2,1:T(8,128)(2,1)} %bitcast.387, pred[320,1280]{1,0:T(8,128)(4,1)S(1)} %copy-done.26), kind=kOutput, calls=%fused_computation.231 | convolution fusion | flops 806088000 | bytes 26438400 | tf_op jit(solution)/shard_map/while/body/eval_jaxpr/qkgd,tkd->kgqt/dot_general | solution.py:52
  207.2 12.3 %fusion.7 = f32[5,3,320]{2,1,0:T(4,128)S(1)} fusion(f32[5,3,320,1280]{3,2,1,0:T(8,128)} %get-tuple-element.180, f32[5,3,320]{2,1,0:T(4,128)} %get-tuple-element.179), kind=kLoop, calls=%fused_computation.19 | loop fusion | flops 12283200 | bytes 24614400 | tf_op jit(solution)/shard_map/while/body/eval_jaxpr/reduce_sum | solution.py:61
  252.1 9.8 fusion.28
  262.0 19.4 %fusion.3 = (f32[5,3,320]{2,1,0:T(4,128)S(1)}, f32[5,1280,320,3]{1,2,3,0:T(8,128)}) fusion(f32[5,3,320,1280]{3,2,1,0:T(8,128)} %get-tuple-element.180, f32[5,3,320]{2,1,0:T(4,128)S(1)} %copy-done.66, bf16[1280,5,64,1]{0,2,3,1:T(8,128)(2,1)S(1)} %bitcast.394, bf16[320,5,3,64]{0,3,2,1:T(8,128)(2,1)S(1)} %bitcast.372), kind=kOutput, calls=%fused_computation.7 | convolution fusion | flops 804859200 | bytes 50624000 | tf_op jit(solution)/shard_map/while/body/eval_jaxpr/qkgd,tkd->kgqt/dot_general | solution.py:73
  281.4 16.4 %fusion.5 = bf16[5,3,320,1280]{3,2,1,0:T(8,128)(2,1)S(1)} fusion(f32[5,1280,320,3]{1,2,3,0:T(8,128)} %get-tuple-element.185, f32[5,3,320,1280]{3,2,1,0:T(8,128)} %get-tuple-element.180, f32[5,3,320]{2,1,0:T(4,128)S(1)} %get-tuple-element.184, f32[5,3,320]{2,1,0:T(4,128)S(1)} %copy-done.66), kind=kLoop, calls=%fused_computation.9 | loop fusion | flops 24576000 | bytes 61478400 | tf_op jit(solution)/shard_map/while/body/eval_jaxpr/convert_element_type | solution.py:77
  324.9 18.4 %reduce-scatter.33.cloned.1.call-done = bf16[320,640]{1,0:T(8,128)(2,1)} async-done(((bf16[1280,640]{1,0:T(8,128)(2,1)}), bf16[320,640]{1,0:T(8,128)(2,1)}) %reduce-scatter.33.cloned.1.call-update) | async-done | bytes 409616
  371.9 9.8 fusion.31
  381.7 19.4 %fusion = (f32[5,3,320]{2,1,0:T(4,128)S(1)}, f32[5,1280,320,3]{1,2,3,0:T(8,128)}) fusion(f32[5,3,320,1280]{3,2,1,0:T(8,128)} %get-tuple-element.172, f32[5,3,320]{2,1,0:T(4,128)S(1)} %copy-done.65, bf16[1280,5,64,1]{0,2,3,1:T(8,128)(2,1)S(1)} %bitcast.392, bf16[320,5,3,64]{0,3,2,1:T(8,128)(2,1)S(1)} %bitcast.374), kind=kOutput, calls=%fused_computation.2 | convolution fusion | flops 804859200 | bytes 50624000 | tf_op jit(solution)/shard_map/while/body/eval_jaxpr/qkgd,tkd->kgqt/dot_general | solution.py:73
  401.1 16.4 %fusion.2 = bf16[5,3,320,1280]{3,2,1,0:T(8,128)(2,1)S(1)} fusion(f32[5,1280,320,3]{1,2,3,0:T(8,128)} %get-tuple-element.189, f32[5,3,320,1280]{3,2,1,0:T(8,128)} %get-tuple-element.172, f32[5,3,320]{2,1,0:T(4,128)S(1)} %get-tuple-element.188, f32[5,3,320]{2,1,0:T(4,128)S(1)} %copy-done.65), kind=kLoop, calls=%fused_computation.4 | loop fusion | flops 24576000 | bytes 61478400 | tf_op jit(solution)/shard_map/while/body/eval_jaxpr/convert_element_type | solution.py:77
  437.8 9.0 convolution_multiply_fusion
  533.5 134.0 %all-reduce.15 = (bf16[960]{0:T(1024)(128)(2,1)S(1)}, bf16[960,320]{0,1:T(8,128)(2,1)S(1)}, bf16[960,320]{0,1:T(8,128)(2,1)}, bf16[960]{0:T(1024)(128)(2,1)S(1)}) all-reduce(f32[960]{0:T(1024)S(1)} %add.284, f32[960,320]{0,1:T(8,128)} %convolution_add_fusion.5, ...), channel_id=4, replica_groups=mesh['seq'=4,'dp'=8] {'dp'}, use_global_device_ids=true, to_apply=%region_18.19.clone | all-reduce | flops 616320 | bytes 3697920
  670.9 23.2 %reduce-scatter.31.cloned.1.call-done = f32[120,960]{1,0:T(8,128)} async-done(((f32[960,960]{1,0:T(8,128)}), f32[120,960]{1,0:T(8,128)}) %reduce-scatter.31.cloned.1.call-update) | async-done | bytes 460816 | tf_op jit(solution)/shard_map/reduce_scatter | solution.py:303
  696.0 51.7 %reduce-scatter.37.cloned.1.call-done = bf16[640,960]{1,0:T(8,128)(2,1)} async-done(((bf16[2560,960]{1,0:T(8,128)(2,1)}), bf16[640,960]{1,0:T(8,128)(2,1)}) %reduce-scatter.37.cloned.1.call-update) | async-done | bytes 1228816
  753.0 48.8 %reduce-scatter.39.cloned.1.call-done = bf16[640,960]{1,0:T(8,128)(2,1)} async-done(((bf16[2560,960]{1,0:T(8,128)(2,1)}), bf16[640,960]{1,0:T(8,128)(2,1)}) %reduce-scatter.39.cloned.1.call-update) | async-done | bytes 1228816
  807.1 48.4 %reduce-scatter.41.cloned.1.call-done = bf16[640,960]{1,0:T(8,128)(2,1)} async-done(((bf16[2560,960]{1,0:T(8,128)(2,1)}), bf16[640,960]{1,0:T(8,128)(2,1)}) %reduce-scatter.41.cloned.1.call-update) | async-done | bytes 1228816
  877.4 15.7 %all-reduce.14.cloned.1.call-done = (bf16[120,960]{1,0:T(8,128)(2,1)}, bf16[120,320]{0,1:T(8,128)(2,1)}, bf16[120,320]{0,1:T(8,128)(2,1)}, bf16[120,960]{1,0:T(8,128)(2,1)}) async-done(((bf16[120,960]{1,0:T(8,128)(2,1)}, bf16[120,320]{0,1:T(8,128)(2,1)}, bf16[120,320]{0,1:T(8,128)(2,1)}, bf16[120,960]{1,0:T(8,128)(2,1)}), (bf16[120,960]{1,0:T(8,128)(2,1)}, bf16[120,320]{0,1:T(8,128)(2,1)}, ...) | async-done | bytes 614416 | tf_op jit(solution)/shard_map/psum | solution.py:311
  899.8 67.6 %reduce-scatter.43.cloned.1.call-done = f32[120,640]{1,0:T(8,128)} async-done(((f32[960,640]{1,0:T(8,128)}), f32[120,640]{1,0:T(8,128)}) %reduce-scatter.43.cloned.1.call-update) | async-done | bytes 307216
  967.4 73.3 %reduce-scatter.45.cloned.1.call-done = f32[120,640]{1,0:T(8,128)} async-done(((f32[960,640]{1,0:T(8,128)}), f32[120,640]{1,0:T(8,128)}) %reduce-scatter.45.cloned.1.call-update) | async-done | bytes 307216
  1040.6 73.2 %reduce-scatter.47.cloned.1.call-done = f32[640,120]{0,1:T(8,128)} async-done(((f32[640,960]{0,1:T(8,128)}), f32[640,120]{0,1:T(8,128)}) %reduce-scatter.47.cloned.1.call-update) | async-done | bytes 307216
  (394 shorter events, 324.2 us)
Async XLA Ops:
  7.2 74.2 %copy-start = (bf16[960,960]{1,0:T(8,128)(2,1)S(1)}, bf16[960,960]{1,0:T(8,128)(2,1)}, u32[]{:S(2)}) copy-start(bf16[960,960]{1,0:T(8,128)(2,1)} %param.20) | copy-start | bytes 5529604
  7.2 30.5 %all-gather.6.cloned.1.call-start = ((), (), s32[]{:S(2)}) async-start(), calls=%async_computation.10 | async-start | bytes 2048000 | tf_op jit(solution)/shard_map/all_gather | solution.py:144
  13.4 157.7 %copy-start.35 = (f32[320,32]{0,1:T(8,128)}, f32[320,32]{0,1:T(8,128)S(1)}, u32[]{:S(2)}) copy-start(f32[320,32]{0,1:T(8,128)S(1)} %get-tuple-element.162) | copy-start | bytes 122884
  14.7 70.1 %all-gather.8.cloned.1.call-start = ((), (), s32[]{:S(2)}) async-start(), calls=%async_computation.11 | async-start | bytes 6144000 | tf_op jit(solution)/shard_map/all_gather | solution.py:123
  15.4 102.6 %all-gather.10.cloned.1.call-start = ((), (), s32[]{:S(2)}) async-start(), calls=%async_computation.12 | async-start | bytes 6144000 | tf_op jit(solution)/shard_map/all_gather | solution.py:124
  16.2 141.8 %all-gather.12.cloned.1.call-start = ((), (), s32[]{:S(2)}) async-start(), calls=%async_computation.13 | async-start | bytes 6144000 | tf_op jit(solution)/shard_map/all_gather | solution.py:125
  16.7 171.8 %all-gather.14.cloned.1.call-start = ((), (), s32[]{:S(2)}) async-start(), calls=%async_computation.14 | async-start | bytes 2048000 | tf_op jit(solution)/shard_map/all_gather | solution.py:144
  92.2 65.8 %copy-start.13 = (f32[1,320,960]{2,1,0:T(8,128)S(1)}, f32[1,320,960]{2,1,0:T(8,128)}, u32[]{:S(2)}) copy-start(f32[1,320,960]{2,1,0:T(8,128)} %copy-done.12) | copy-start | bytes 3686404
  168.4 174.9 %reduce-scatter.33.cloned.1.call-start = ((), (), s32[]{:S(2)}) async-start(), calls=%async_computation.17 | async-start | bytes 2048000
  281.4 16.4 %copy-start.40 = (bf16[1,320,15,32]{1,3,2,0:T(8,128)(2,1)S(1)}, bf16[1,320,15,32]{1,3,2,0:T(8,128)(2,1)}, u32[]{:S(2)}) copy-start(bf16[1,320,15,32]{1,3,2,0:T(8,128)(2,1)} %get-tuple-element.144) | copy-start | bytes 921604
  281.4 16.4 %copy-start.41 = (bf16[1,320,15,32]{1,3,2,0:T(8,128)(2,1)S(1)}, bf16[1,320,15,32]{1,3,2,0:T(8,128)(2,1)}, u32[]{:S(2)}) copy-start(bf16[1,320,15,32]{1,3,2,0:T(8,128)(2,1)} %get-tuple-element.145) | copy-start | bytes 921604
  314.5 201.0 %reduce-scatter.35.cloned.1.call-start = ((), (), s32[]{:S(2)}) async-start(), calls=%async_computation.18 | async-start | bytes 2048000
  324.9 28.7 %copy-start.47 = (bf16[1,320,15,64]{1,3,2,0:T(8,128)(2,1)}, bf16[1,320,15,64]{1,3,2,0:T(8,128)(2,1)S(1)}, u32[]{:S(2)}) copy-start(bf16[1,320,15,64]{1,3,2,0:T(8,128)(2,1)S(1)} %maximum_convert_fusion) | copy-start | bytes 1843204
  401.1 16.4 %copy-start.38 = (bf16[1,320,15,32]{1,3,2,0:T(8,128)(2,1)S(1)}, bf16[1,320,15,32]{1,3,2,0:T(8,128)(2,1)}, u32[]{:S(2)}) copy-start(bf16[1,320,15,32]{1,3,2,0:T(8,128)(2,1)} %get-tuple-element.146) | copy-start | bytes 921604
  401.1 16.4 %copy-start.39 = (bf16[1,320,15,32]{1,3,2,0:T(8,128)(2,1)S(1)}, bf16[1,320,15,32]{1,3,2,0:T(8,128)(2,1)}, u32[]{:S(2)}) copy-start(bf16[1,320,15,32]{1,3,2,0:T(8,128)(2,1)} %get-tuple-element.147) | copy-start | bytes 921604
  434.3 234.9 %reduce-scatter.29.cloned.1.call-start = ((), (), s32[]{:S(2)}) async-start(), calls=%async_computation.15 | async-start | bytes 4423680 | tf_op jit(solution)/shard_map/reduce_scatter | solution.py:300
  451.5 242.6 %reduce-scatter.31.cloned.1.call-start = ((), (), s32[]{:S(2)}) async-start(), calls=%async_computation.16 | async-start | bytes 4423680 | tf_op jit(solution)/shard_map/reduce_scatter | solution.py:303
  457.6 290.0 %reduce-scatter.37.cloned.1.call-start = ((), (), s32[]{:S(2)}) async-start(), calls=%async_computation.19 | async-start | bytes 6553600
  475.1 326.6 %reduce-scatter.39.cloned.1.call-start = ((), (), s32[]{:S(2)}) async-start(), calls=%async_computation.20 | async-start | bytes 6553600
  492.3 363.2 %reduce-scatter.41.cloned.1.call-start = ((), (), s32[]{:S(2)}) async-start(), calls=%async_computation.21 | async-start | bytes 6553600
  509.6 383.5 %all-reduce.14.cloned.1.call-start = ((), (), s32[]{:S(2)}) async-start(), calls=%async_computation.25 | async-start | bytes 1310720 | tf_op jit(solution)/shard_map/psum | solution.py:311
  695.9 271.5 %reduce-scatter.43.cloned.1.call-start = ((), (), s32[]{:S(2)}) async-start(), calls=%async_computation.22 | async-start | bytes 2764800
  752.9 287.7 %reduce-scatter.45.cloned.1.call-start = ((), (), s32[]{:S(2)}) async-start(), calls=%async_computation.23 | async-start | bytes 2764800
  807.1 306.8 %reduce-scatter.47.cloned.1.call-start = ((), (), s32[]{:S(2)}) async-start(), calls=%async_computation.24 | async-start | bytes 2764800
  (97 other events, 418.2 us)
Sparse Core Ops, SparseCore 0:
  14.8 22.8 all-gather.5
  39.3 38.5 all-gather.7
  79.4 38.5 all-gather.9
  119.4 38.5 all-gather.11
  168.5 20.0 all-gather.13
  314.7 28.5 reduce-scatter.32
  434.4 28.5 reduce-scatter.34
  466.7 89.4 reduce-scatter.28
  560.3 133.7 reduce-scatter.30
  696.5 51.0 reduce-scatter.36
  750.4 51.3 reduce-scatter.38
  804.1 51.3 reduce-scatter.40
  858.8 34.2 all-reduce.13
  897.6 69.7 reduce-scatter.42
  971.9 68.7 reduce-scatter.44
  1045.1 68.6 reduce-scatter.46
where the time goes:
time: 1130 us; the launch traced here: 1120 us
  waiting for transfers between devices  501 us (44%)
  matrix products  243 us (22%)
  blocking collectives  147 us (13%)
  local copies, waits for them, and re-layouts  111 us (10%)
  other arithmetic  100 us (9%)
  between operations  17.3 us (2%)
    unnamed x24, waiting for transfers between devices  383 us
    unnamed x2, blocking collectives  141 us
    unnamed x233, local copies, waits for them, and re-layouts  88.9 us
    dot_general x2, matrix products, row_backward(): jnp.einsum('qkgd,tkd->kgqt', mixed_grad, values_all, preferred_element_ty...  38.8 us
    convert_element_type x2, other arithmetic, row_backward(): score_grad = (weights_soft * (probs_grad - row_delta)).astype(jnp.bfloat16)  32.7 us
    all_gather x1, waiting for transfers between devices, on_device(): lax.all_gather(w_down, 'seq', axis=0, tiled=True)  32.2 us
    dot_general x2, matrix products, masked_scores(): jnp.einsum('qkgd,tkd->kgqt', queries, keys_all, preferred_element_type=jn...  26.1 us
    all_gather x1, waiting for transfers between devices, on_device(): lax.all_gather(w_up, 'seq', axis=1, tiled=True)  25.8 us
  transfers between devices with their start and end apart: 16, of which 13 were waited for; matrix products, arithmetic and copies ran while one was open for 19% of the time, Pallas kernels for 0%

commit v1 on v0

--- a/solution.py
+++ b/solution.py
@@ -1,7 +1,13 @@
+import functools
+
 import jax
 import jax.numpy as jnp
 from jax import lax
+from jax.experimental import pallas as pl
+from jax.experimental.pallas import tpu as pltpu
 from jax.sharding import PartitionSpec as P
+
+MESH_ID = pl.DeviceIdType.MESH
 
 HEADS = 15
 KV_HEADS = 5
@@ -91,6 +97,153 @@
         preferred_element_type=jnp.float32,
     )
     return (query_grad, key_grad, value_grad)
+
+
+def device(seq_pos, dp_pos):
+    return {"seq": seq_pos, "dp": dp_pos}
+
+
+def send(src, dst, send_sem, recv_sem, target):
+    copy = pltpu.make_async_remote_copy(
+        src_ref=src,
+        dst_ref=dst,
+        send_sem=send_sem,
+        recv_sem=recv_sem,
+        device_id=target,
+        device_id_type=MESH_ID,
+    )
+    copy.start()
+    return copy
+
+
+def greet(targets):
+    barrier = pltpu.get_barrier_semaphore()
+    for target in targets:
+        pl.semaphore_signal(barrier, inc=1, device_id=target, device_id_type=MESH_ID)
+    pl.semaphore_wait(barrier, len(targets))
+
+
+def reduce_kernel(
+    attn_ref, ffn_ref, gain_ref,
+    attn_out, ffn_out, gain_out,
+    core_send, core_recv, x_send, x_recv, own,
+    y_send, y_recv, z_send, z_recv, g_recv, share_low,
+    send_sem, recv_sem,
+):
+    seq, dp = lax.axis_index("seq"), lax.axis_index("dp")
+    core, chip_x = lax.rem(seq, 2), lax.div(seq, 2)
+    row_y, row_z = lax.rem(dp, 2), lax.div(dp, 2)
+    mate = device(seq + 1 - 2 * core, dp)
+    x_mate = device(lax.rem(seq + 2, 4), dp)
+    y_mate = device(seq, dp + 1 - 2 * row_y)
+    z_of = [lax.rem(row_z + k, 4) for k in range(1, 4)]
+    z_mates = [device(seq, z * 2 + row_y) for z in z_of]
+    greet([mate, x_mate, y_mate] + z_mates)
+    low = jnp.bfloat16
+
+    def y_start(index, load):
+        for z in range(4):
+            y_send[index, z] = load(2 * z + 1 - row_y).astype(low)
+        return send(y_send.at[index], y_recv.at[index], send_sem.at[index], recv_sem.at[index], y_mate)
+
+    def z_start(index, load):
+        copies = []
+        for k in range(3):
+            z = z_of[k]
+            z_send[index, k] = (load(2 * z + row_y) + y_recv[index, z].astype(jnp.float32)).astype(low)
+            sem = 4 + 3 * index + k
+            copies.append(
+                send(z_send.at[index, k], z_recv.at[index, k], send_sem.at[sem], recv_sem.at[sem], z_mates[k])
+            )
+        return copies
+
+    def z_finish(index, load, copies):
+        total = load(2 * row_z + row_y) + y_recv[index, row_z].astype(jnp.float32)
+        for k in range(3):
+            copies[k].wait()
+            total = total + z_recv[index, k].astype(jnp.float32)
+        return total
+
+    gain_out[...] = gain_ref[...]
+    hops = [mate, x_mate, y_mate, device(seq, lax.rem(dp + 4, 8)), device(seq, dp + 2 - 4 * lax.rem(row_z, 2))]
+
+    def gain_start(hop):
+        sem = 22 + hop
+        return send(gain_ref if hop == 0 else gain_out, g_recv.at[hop], send_sem.at[sem], recv_sem.at[sem], hops[hop])
+
+    for half in range(2):
+        core_send[half] = attn_ref[2 * half + 1 - core].astype(low)
+    core_copy = send(core_send, core_recv, send_sem.at[16], recv_sem.at[16], mate)
+    gain_copy = gain_start(0)
+    ffn_load = lambda m: (lambda j: ffn_ref[m, j])
+    y_copies = [y_start(m, ffn_load(m)) for m in range(3)]
+    core_copy.wait()
+    x_send[...] = (
+        attn_ref[2 * (1 - chip_x) + core] + core_recv[1 - chip_x].astype(jnp.float32)
+    ).astype(low)
+    x_copy = send(x_send, x_recv, send_sem.at[17], recv_sem.at[17], x_mate)
+    own[...] = attn_ref[seq] + core_recv[chip_x].astype(jnp.float32)
+    for hop in range(5):
+        gain_copy.wait()
+        gain_out[...] += g_recv[hop]
+        if hop < 4:
+            gain_copy = gain_start(hop + 1)
+    z_copies = []
+    for m in range(3):
+        y_copies[m].wait()
+        z_copies.append(z_start(m, ffn_load(m)))
+    x_copy.wait()
+    own[...] += x_recv[...].astype(jnp.float32)
+    own_load = lambda j: own[j]
+    y_copy = y_start(3, own_load)
+    for m in range(3):
+        ffn_out[m] = z_finish(m, ffn_load(m), z_copies[m])
+    y_copy.wait()
+    z_copy = z_start(3, own_load)
+    share_low[seq] = z_finish(3, own_load, z_copy).astype(low)
+    to_mate = send(share_low.at[seq], share_low.at[seq], send_sem.at[18], recv_sem.at[18], mate)
+    to_x = send(share_low.at[seq], share_low.at[seq], send_sem.at[19], recv_sem.at[19], x_mate)
+    to_x.wait()
+    far = lax.rem(seq + 2, 4)
+    onward = send(share_low.at[far], share_low.at[far], send_sem.at[20], recv_sem.at[20], mate)
+    to_mate.wait()
+    onward.wait()
+    attn_out[...] = share_low[...].astype(jnp.float32)
+
+
+def reduce_grads(attn_grads, ffn_grads, gain_grads):
+    share, cols = attn_grads.shape[2:]
+    low, full = jnp.bfloat16, jnp.float32
+    vmem = pl.BlockSpec(memory_space=pltpu.VMEM)
+    return pl.pallas_call(
+        reduce_kernel,
+        out_shape=(
+            jax.ShapeDtypeStruct((4, share, cols), full),
+            jax.ShapeDtypeStruct((3, share, cols), full),
+            jax.ShapeDtypeStruct(gain_grads.shape, full),
+        ),
+        in_specs=[vmem] * 3,
+        out_specs=(vmem, vmem, vmem),
+        scratch_shapes=[
+            pltpu.VMEM((2, 8, share, cols), low),
+            pltpu.VMEM((2, 8, share, cols), low),
+            pltpu.VMEM((8, share, cols), low),
+            pltpu.VMEM((8, share, cols), low),
+            pltpu.VMEM((8, share, cols), full),
+            pltpu.VMEM((4, 4, share, cols), low),
+            pltpu.VMEM((4, 4, share, cols), low),
+            pltpu.VMEM((4, 3, share, cols), low),
+            pltpu.VMEM((4, 3, share, cols), low),
+            pltpu.VMEM((5,) + gain_grads.shape, full),
+            pltpu.VMEM((4, share, cols), low),
+            pltpu.SemaphoreType.DMA((27,)),
+            pltpu.SemaphoreType.DMA((27,)),
+        ],
+        compiler_params=pltpu.CompilerParams(
+            collective_id=0, has_side_effects=True, vmem_limit_bytes=60 * 1024 * 1024
+        ),
+        name="reduce_grads",
+    )(attn_grads, ffn_grads, gain_grads)
 
 
 def on_device(
@@ -119,11 +272,7 @@
         key_place[None, None, :] <= query_place[None, :, None]
     )
     cos_table, sin_table = rope_tables(positions)
-    gate_mat, up_mat, down_mat = (
-        lax.all_gather(w_gate, "seq", axis=1, tiled=True),
-        lax.all_gather(w_up, "seq", axis=1, tiled=True),
-        lax.all_gather(w_down, "seq", axis=0, tiled=True),
-    )
+    gate_mat, up_mat, down_mat = w_gate, w_up, w_down
     residual = tokens.astype(jnp.float32)
     kept_runs = []
     for repeat in range(2):
@@ -151,6 +300,7 @@
             "rce,ed->rcd", mixed_low, w_out, preferred_element_type=jnp.float32
         )
         normed_two, ffn_inverse = norm_forward(after_attn, ffn_gain)
+        normed_two = lax.all_gather(normed_two, "seq", axis=1, tiled=True)
         gate_pre = jnp.einsum(
             "rtd,df->rtf", normed_two, gate_mat, preferred_element_type=jnp.float32
         )
@@ -159,6 +309,9 @@
         partial_sum = jnp.einsum(
             "rtf,fd->rtd", ffn_hidden, down_mat, preferred_element_type=jnp.float32
         )
+        partial_sum = lax.psum_scatter(
+            partial_sum.astype(jnp.bfloat16), "seq", scatter_dimension=1, tiled=True
+        ).astype(jnp.float32)
         normed_rows, gate_pre, up_pre, ffn_out = (normed_two, gate_pre, up_pre, partial_sum)
         kept_runs.append(
             (
@@ -187,7 +340,7 @@
     w_out_grad = jnp.zeros(w_out.shape, jnp.float32)
     w_gate_grad = jnp.zeros(gate_mat.shape, jnp.float32)
     w_up_grad = jnp.zeros(up_mat.shape, jnp.float32)
-    w_down_grad = jnp.zeros(down_mat.shape, jnp.float32)
+    w_down_grad = jnp.zeros(down_mat.shape[::-1], jnp.float32)
     upstream = cotangent.astype(jnp.float32)
     for repeat in (1, 0):
         (
@@ -205,12 +358,12 @@
             gate_pre,
             up_pre,
         ) = kept_runs[repeat]
-        ffn_grad = upstream.astype(jnp.bfloat16)
+        ffn_grad = lax.all_gather(upstream.astype(jnp.bfloat16), "seq", axis=1, tiled=True)
         sigmoid_gate = jax.nn.sigmoid(gate_pre)
         silu_gate = jax.nn.silu(gate_pre)
         hidden = (silu_gate * up_pre).astype(jnp.bfloat16)
         w_down_grad = w_down_grad + jnp.einsum(
-            "rtf,rtd->fd", hidden, ffn_grad, preferred_element_type=jnp.float32
+            "rtf,rtd->df", hidden, ffn_grad, preferred_element_type=jnp.float32
         )
         hidden_grad = jnp.einsum(
             "rtd,fd->rtf", ffn_grad, down_mat, preferred_element_type=jnp.float32
@@ -228,6 +381,9 @@
         normed_two_grad = jnp.einsum(
             "rtf,df->rtd", gate_grad, gate_mat, preferred_element_type=jnp.float32
         ) + jnp.einsum("rtf,df->rtd", up_grad, up_mat, preferred_element_type=jnp.float32)
+        normed_two_grad = lax.psum_scatter(
+            normed_two_grad.astype(jnp.bfloat16), "seq", scatter_dimension=1, tiled=True
+        ).astype(jnp.float32)
         after_grad, gain_two = norm_backward(after_attn, ffn_inverse, ffn_gain, normed_two_grad)
         after_grad = after_grad + upstream
         ffn_gain_grad = ffn_gain_grad + gain_two
@@ -284,48 +440,52 @@
         residual_grad, gain_one = norm_backward(residual, attn_inverse, attn_gain, normed_grad)
         attn_gain_grad = attn_gain_grad + gain_one
         upstream = residual_grad + after_grad
-    w_gate_grad, w_up_grad, w_down_grad = (
-        lax.psum_scatter(
-            w_gate_grad.astype(jnp.bfloat16), "seq", scatter_dimension=1, tiled=True
-        ).astype(jnp.float32),
-        lax.psum_scatter(
-            w_up_grad.astype(jnp.bfloat16), "seq", scatter_dimension=1, tiled=True
-        ).astype(jnp.float32),
-        lax.psum_scatter(
-            w_down_grad.astype(jnp.bfloat16), "seq", scatter_dimension=0, tiled=True
-        ).astype(jnp.float32),
-    )
-    shards = (
-        lax.psum_scatter(attn_gain_grad, "dp", scatter_dimension=0, tiled=True),
-        lax.psum_scatter(w_query_grad, "dp", scatter_dimension=0, tiled=True),
-        lax.psum_scatter(w_key_grad, "dp", scatter_dimension=0, tiled=True),
-        lax.psum_scatter(w_value_grad, "dp", scatter_dimension=0, tiled=True),
-        lax.psum_scatter(w_out_grad, "dp", scatter_dimension=0, tiled=True),
-        lax.psum_scatter(ffn_gain_grad, "dp", scatter_dimension=0, tiled=True),
-        lax.psum_scatter(w_gate_grad, "dp", scatter_dimension=0, tiled=True),
-        lax.psum_scatter(w_up_grad, "dp", scatter_dimension=0, tiled=True),
-        lax.psum_scatter(w_down_grad, "dp", scatter_dimension=1, tiled=True),
-    )
-    attn_sums = (
-        lax.psum(shards[0].astype(jnp.bfloat16), "seq").astype(jnp.float32),
-        lax.psum(shards[1].astype(jnp.bfloat16), "seq").astype(jnp.float32),
-        lax.psum(shards[2].astype(jnp.bfloat16), "seq").astype(jnp.float32),
-        lax.psum(shards[3].astype(jnp.bfloat16), "seq").astype(jnp.float32),
-        lax.psum(shards[4].astype(jnp.bfloat16), "seq").astype(jnp.float32),
-        lax.psum(shards[5].astype(jnp.bfloat16), "seq").astype(jnp.float32),
-    )
+    if lax.axis_size("dp") == 8 and lax.axis_size("seq") == 4 and model_width % 64 == 0:
+        share = model_width // 8
+        attn_grads = jnp.concatenate([w_query_grad, w_key_grad, w_value_grad, w_out_grad], axis=1)
+        attn_grads = attn_grads.reshape(8, share, 4, -1).transpose(2, 0, 1, 3)
+        ffn_grads = jnp.stack([w_gate_grad, w_up_grad, w_down_grad]).reshape(3, 8, share, -1)
+        gain_grads = jnp.stack([attn_gain_grad, ffn_gain_grad]).reshape(2, 8, share).transpose(1, 0, 2)
+        gain_grads = jnp.pad(gain_grads, ((0, 0), (0, 6), (0, 128 - share)))
+        attn_share, ffn_share, gain_share = reduce_grads(attn_grads, ffn_grads, gain_grads)
+        attn_share = attn_share.transpose(1, 0, 2).reshape(share, -1)
+        own_gains = lax.dynamic_index_in_dim(gain_share, lax.axis_index("dp"), 0, keepdims=False)
+        q_end = w_query.shape[1]
+        k_end = q_end + w_key.shape[1]
+        v_end = k_end + w_value.shape[1]
+        return (
+            output,
+            upstream,
+            own_gains[0, :share],
+            attn_share[:, :q_end],
+            attn_share[:, q_end:k_end],
+            attn_share[:, k_end:v_end],
+            attn_share[:, v_end:],
+            own_gains[1, :share],
+            ffn_share[0],
+            ffn_share[1],
+            ffn_share[2].T,
+        )
+
+    def over_rows(grad):
+        low_grad = grad.astype(jnp.bfloat16)
+        return lax.psum_scatter(low_grad, "dp", scatter_dimension=0, tiled=True).astype(jnp.float32)
+
+    def over_all(grad):
+        return lax.psum(over_rows(grad).astype(jnp.bfloat16), "seq").astype(jnp.float32)
+
     return (
         output,
         upstream,
-        attn_sums[0],
-        attn_sums[1],
-        attn_sums[2],
-        attn_sums[3],
-        attn_sums[4],
-        attn_sums[5],
-        shards[6],
-        shards[7],
-        shards[8],
+        over_all(attn_gain_grad),
+        over_all(w_query_grad),
+        over_all(w_key_grad),
+        over_all(w_value_grad),
+        over_all(w_out_grad),
+        over_all(ffn_gain_grad),
+        over_rows(w_gate_grad),
+        over_rows(w_up_grad),
+        over_rows(w_down_grad).T,
     )
 
 

time: 1130 us -> 915 us (0.81)
  waiting for transfers between devices: 501 us -> 226 us
  blocking collectives: 147 us -> 6.41 us
  Pallas kernels: 0 us -> 115 us
  local copies, waits for them, and re-layouts: 111 us -> 206 us
  other arithmetic: 100 us -> 87.1 us
    unnamed x24 -> x18, waiting for transfers between devices: 383 us -> 111 us
    unnamed x2 -> x1, blocking collectives: 141 us -> 6.41 us
    pallas_call x0 -> x1, Pallas kernels: none -> 115 us  [reduce_grads(): pl.pallas_call(reduce_kernel, out_shape=(jax.ShapeDtypeStruct((4, share,...]
    unnamed x233 -> x220, local copies, waits for them, and re-layouts: 88.9 us -> 137 us
    all_gather x3 -> x4, waiting for transfers between devices: 58.1 us -> 92.8 us  [the longest x2 50.1 us: on_device(): normed_two = lax.all_gather(normed_two, 'seq', axis=1, tiled=True)]
    reduce_scatter x2 -> x0, waiting for transfers between devices: 23.2 us -> none  [the longest x1 23.2 us: on_device(): lax.psum_scatter(w_out_grad, 'dp', scatter_dimension=0, tiled=True)]
    reshape x0 -> x3, local copies, waits for them, and re-layouts: none -> 22 us  [the longest x2 20.6 us: on_device(): attn_grads = attn_grads.reshape(8, share, 4, -1).transpose(2, 0, 1, 3)]
    convert_element_type x11 -> x1, other arithmetic: 19.9 us -> 1.69 us  [on_device(): upstream.astype(jnp.bfloat16)]
  transfers between devices with their start and end apart: 16 -> 12, of which waited for: 13 -> 12; matrix products, arithmetic and copies ran while one was open for 19% -> 12% of each run, Pallas kernels for 0% -> 0%
where the time goes in v1:
time: 915 us; the launch traced here: 902 us
  matrix products  243 us (27%)
  waiting for transfers between devices  226 us (25%)
  local copies, waits for them, and re-layouts  206 us (23%)
  Pallas kernels  115 us (13%)
  other arithmetic  87.1 us (10%)
  between operations  16.3 us (2%)
    unnamed x220, local copies, waits for them, and re-layouts  137 us
    pallas_call x1, Pallas kernels, reduce_grads(): pl.pallas_call(reduce_kernel, out_shape=(jax.ShapeDtypeStruct((4, share,...  115 us
    unnamed x18, waiting for transfers between devices  111 us
    all_gather x2, waiting for transfers between devices, on_device(): normed_two = lax.all_gather(normed_two, 'seq', axis=1, tiled=True)  50.1 us
    all_gather x2, waiting for transfers between devices, on_device(): lax.all_gather(upstream.astype(jnp.bfloat16), 'seq', axis=1, tiled=True)  42.8 us
    dot_general x2, matrix products, row_backward(): jnp.einsum('qkgd,tkd->kgqt', mixed_grad, values_all, preferred_element_ty...  39.4 us
    convert_element_type x2, other arithmetic, row_backward(): score_grad = (weights_soft * (probs_grad - row_delta)).astype(jnp.bfloat16)  32.7 us
    dot_general x2, matrix products, masked_scores(): jnp.einsum('qkgd,tkd->kgqt', queries, keys_all, preferred_element_type=jn...  23.4 us
  transfers between devices with their start and end apart: 12, of which 12 were waited for; matrix products, arithmetic and copies ran while one was open for 12% of the time, Pallas kernels for 0%

profile of v1, /device:TPU:0, one launch (start us, length us, event | category | flops | bytes accessed | tf_op | source)
XLA Modules:
  0.0 902.0 jit_solution(4682001619922204630)
XLA Ops:
  47.5 11.7 %fusion.152 = (f32[5,3,320]{2,1,0:T(4,128)S(1)}, f32[5,3,320,1280]{3,2,1,0:T(8,128)}) fusion(bf16[1280,5,64,1]{0,2,3,1:T(8,128)(2,1)S(1)} %bitcast.398, bf16[320,5,3,32]{0,3,2,1:T(8,128)(2,1)} %bitcast.424, bf16[320,5,3,32]{0,3,2,1:T(8,128)(2,1)} %bitcast.422, pred[320,1280]{1,0:T(8,128)(4,1)S(1)} %fusion.66), kind=kOutput, calls=%fused_computation.266 | convolution fusion | flops 806088000 | bytes 26438400 | tf_op jit(solution)/shard_map/while/body/eval_jaxpr/qkgd,tkd->kgqt/dot_general | solution.py:58
  59.2 11.4 %fusion.6 = f32[5,3,320]{2,1,0:T(4,128)S(1)} fusion(f32[5,3,320,1280]{3,2,1,0:T(8,128)} %get-tuple-element.238, f32[5,3,320]{2,1,0:T(4,128)S(1)} %get-tuple-element.237), kind=kLoop, calls=%fused_computation.18 | loop fusion | flops 12283200 | bytes 24614400 | tf_op jit(solution)/shard_map/while/body/eval_jaxpr/reduce_sum | solution.py:67
  85.5 25.2 %all-gather.9.cloned.1.call-done = bf16[1,1280,960]{2,1,0:T(8,128)(2,1)} async-done(((bf16[1,320,960]{2,1,0:T(8,128)(2,1)}), bf16[1,1280,960]{2,1,0:T(8,128)(2,1)}) %all-gather.9.cloned.1.call-update) | async-done | bytes 2457616 | tf_op jit(solution)/shard_map/all_gather | solution.py:303
  124.0 11.5 %copy.156 = bf16[1,1280,960]{2,0,1:T(2,128)(2,1)} copy(bf16[1,1280,960]{1,2,0:T(8,128)(2,1)} %fusion.20) | data formatting | bytes 4915200
  140.6 34.8 %reduce-scatter.19.cloned.1.call-done = bf16[320,960]{1,0:T(8,128)(2,1)} async-done(((bf16[1280,960]{1,0:T(8,128)(2,1)}), bf16[320,960]{1,0:T(8,128)(2,1)}) %reduce-scatter.19.cloned.1.call-update) | async-done | bytes 614416
  187.1 16.1 %all-gather.11.cloned.1.call-done = bf16[1,1280,640]{2,1,0:T(8,128)(2,1)} async-done(((bf16[1,320,640]{2,1,0:T(8,128)(2,1)}), bf16[1,1280,640]{2,1,0:T(8,128)(2,1)}) %all-gather.11.cloned.1.call-update) | async-done | bytes 1638416 | tf_op jit(solution)/shard_map/all_gather | solution.py:293
  210.7 11.7 %fusion.153 = (f32[5,3,320]{2,1,0:T(4,128)S(1)}, f32[5,3,320,1280]{3,2,1,0:T(8,128)}) fusion(bf16[1280,5,64,1]{0,2,3,1:T(8,128)(2,1)S(1)} %bitcast.400, bf16[320,5,3,32]{0,3,2,1:T(8,128)(2,1)} %bitcast.428, bf16[320,5,3,32]{0,3,2,1:T(8,128)(2,1)} %bitcast.426, pred[320,1280]{1,0:T(8,128)(4,1)S(1)} %copy-done.27), kind=kOutput, calls=%fused_computation.267 | convolution fusion | flops 806088000 | bytes 26438400 | tf_op jit(solution)/shard_map/while/body/eval_jaxpr/qkgd,tkd->kgqt/dot_general | solution.py:58
  222.4 11.3 %fusion.7 = f32[5,3,320]{2,1,0:T(4,128)S(1)} fusion(f32[5,3,320,1280]{3,2,1,0:T(8,128)} %get-tuple-element.244, f32[5,3,320]{2,1,0:T(4,128)S(1)} %get-tuple-element.243), kind=kLoop, calls=%fused_computation.19 | loop fusion | flops 12283200 | bytes 24614400 | tf_op jit(solution)/shard_map/while/body/eval_jaxpr/reduce_sum | solution.py:67
  248.5 24.9 %all-gather.13.cloned.1.call-done = bf16[1,1280,960]{2,1,0:T(8,128)(2,1)} async-done(((bf16[1,320,960]{2,1,0:T(8,128)(2,1)}), bf16[1,1280,960]{2,1,0:T(8,128)(2,1)}) %all-gather.13.cloned.1.call-update) | async-done | bytes 2457616 | tf_op jit(solution)/shard_map/all_gather | solution.py:303
  283.4 17.1 %all-gather.15.cloned.1.call-done = bf16[1,1280,960]{2,1,0:T(8,128)(2,1)} async-done(((bf16[1,320,960]{2,1,0:T(8,128)(2,1)}), bf16[1,1280,960]{2,1,0:T(8,128)(2,1)}) %all-gather.15.cloned.1.call-update) | async-done | bytes 2457616 | tf_op jit(solution)/shard_map/all_gather | solution.py:361
  314.8 11.6 %copy.160 = bf16[1,1280,960]{2,0,1:T(2,128)(2,1)} copy(bf16[1,1280,960]{1,2,0:T(8,128)(2,1)} %fusion.22) | data formatting | bytes 4915200
  337.4 11.7 %copy.158 = bf16[1,1280,960]{2,0,1:T(2,128)(2,1)} copy(bf16[1,1280,960]{1,2,0:T(8,128)(2,1)} %fusion.21) | data formatting | bytes 4915200
  354.2 12.1 %reduce-scatter.23.cloned.1.call-done = bf16[320,960]{1,0:T(8,128)(2,1)} async-done(((bf16[1280,960]{1,0:T(8,128)(2,1)}), bf16[320,960]{1,0:T(8,128)(2,1)}) %reduce-scatter.23.cloned.1.call-update) | async-done | bytes 614416
  370.1 33.4 %reduce-scatter.21.cloned.1.call-done = bf16[320,960]{1,0:T(8,128)(2,1)} async-done(((bf16[1280,960]{1,0:T(8,128)(2,1)}), bf16[320,960]{1,0:T(8,128)(2,1)}) %reduce-scatter.21.cloned.1.call-update) | async-done | bytes 614416
  411.2 19.7 %fusion.3 = (f32[5,3,320]{2,1,0:T(4,128)S(1)}, f32[5,1280,320,3]{1,2,3,0:T(8,128)}) fusion(f32[5,3,320,1280]{3,2,1,0:T(8,128)} %get-tuple-element.244, f32[5,3,320]{2,1,0:T(4,128)S(1)} %log_add_fusion, bf16[1280,5,64,1]{0,2,3,1:T(8,128)(2,1)} %bitcast.433, bf16[320,5,3,64]{0,3,2,1:T(8,128)(2,1)S(1)} %bitcast.408), kind=kOutput, calls=%fused_computation.7 | convolution fusion | flops 804859200 | bytes 50624000 | tf_op jit(solution)/shard_map/while/body/eval_jaxpr/qkgd,tkd->kgqt/dot_general | solution.py:79
  440.7 16.4 %fusion.5 = bf16[5,3,320,1280]{3,2,1,0:T(8,128)(2,1)S(1)} fusion(f32[5,1280,320,3]{1,2,3,0:T(8,128)} %get-tuple-element.248, f32[5,3,320,1280]{3,2,1,0:T(8,128)} %get-tuple-element.244, f32[5,3,320]{2,1,0:T(4,128)S(1)} %get-tuple-element.247, f32[5,3,320]{2,1,0:T(4,128)S(1)} %log_add_fusion), kind=kLoop, calls=%fused_computation.9 | loop fusion | flops 24576000 | bytes 61478400 | tf_op jit(solution)/shard_map/while/body/eval_jaxpr/convert_element_type | solution.py:83
  484.5 17.9 %reduce-scatter.25.cloned.1.call-done = bf16[320,640]{1,0:T(8,128)(2,1)} async-done(((bf16[1280,640]{1,0:T(8,128)(2,1)}), bf16[320,640]{1,0:T(8,128)(2,1)}) %reduce-scatter.25.cloned.1.call-update) | async-done | bytes 409616
  518.6 25.7 %all-gather.17.cloned.1.call-done = bf16[1,1280,960]{2,1,0:T(8,128)(2,1)} async-done(((bf16[1,320,960]{2,1,0:T(8,128)(2,1)}), bf16[1,1280,960]{2,1,0:T(8,128)(2,1)}) %all-gather.17.cloned.1.call-update) | async-done | bytes 2457616 | tf_op jit(solution)/shard_map/all_gather | solution.py:361
  557.2 11.5 %copy.164 = bf16[1,1280,960]{2,0,1:T(2,128)(2,1)} copy(bf16[1,1280,960]{1,2,0:T(8,128)(2,1)} %fusion.23) | data formatting | bytes 4915200
  616.5 19.7 %fusion = (f32[5,3,320]{2,1,0:T(4,128)S(1)}, f32[5,1280,320,3]{1,2,3,0:T(8,128)}) fusion(f32[5,3,320,1280]{3,2,1,0:T(8,128)} %get-tuple-element.238, f32[5,3,320]{2,1,0:T(4,128)S(1)} %log_add_fusion.1, bf16[1280,5,64,1]{0,2,3,1:T(8,128)(2,1)} %bitcast.431, bf16[320,5,3,64]{0,3,2,1:T(8,128)(2,1)S(1)} %bitcast.410), kind=kOutput, calls=%fused_computation.2 | convolution fusion | flops 804859200 | bytes 50624000 | tf_op jit(solution)/shard_map/while/body/eval_jaxpr/qkgd,tkd->kgqt/dot_general | solution.py:79
  645.9 16.4 %fusion.2 = bf16[5,3,320,1280]{3,2,1,0:T(8,128)(2,1)S(1)} fusion(f32[5,1280,320,3]{1,2,3,0:T(8,128)} %get-tuple-element.251, f32[5,3,320,1280]{3,2,1,0:T(8,128)} %get-tuple-element.238, f32[5,3,320]{2,1,0:T(4,128)S(1)} %get-tuple-element.250, f32[5,3,320]{2,1,0:T(4,128)S(1)} %log_add_fusion.1), kind=kLoop, calls=%fused_computation.4 | loop fusion | flops 24576000 | bytes 61478400 | tf_op jit(solution)/shard_map/while/body/eval_jaxpr/convert_element_type | solution.py:83
  736.0 11.5 %concatenate.133 = f32[960,2560]{1,0:T(8,128)} concatenate(f32[960,960]{1,0:T(8,128)} %convolution_add_fusion.1, f32[960,320]{1,0:T(8,128)} %copy.142, f32[960,320]{1,0:T(8,128)} %copy.143, f32[960,960]{1,0:T(8,128)} %convolution_add_fusion), dimensions={1} | concatenate | bytes 19660800 | tf_op jit(solution)/shard_map/concatenate | solution.py:445
  747.6 12.3 %reshape.979 = f32[8,120,4,640]{3,2,1,0:T(4,128)} reshape(f32[960,2560]{1,0:T(8,128)} %concatenate.133) | data formatting | bytes 19660800 | tf_op jit(solution)/shard_map/reshape | solution.py:446
  768.8 114.5 %reduce_grads.1 = (f32[4,120,640]{2,1,0:T(8,128)}, f32[3,120,640]{2,1,0:T(8,128)}, f32[8,8,128]{2,1,0:T(8,128)}) custom-call(f32[4,8,120,640]{3,2,1,0:T(8,128)} %bitcast.391, f32[3,8,120,640]{3,2,1,0:T(8,128)} %pad_maximum_fusion.ffn_ref, f32[8,8,128]{2,1,0:T(8,128)} %pad.4.gain_ref), custom_call_target="tpu_custom_call" | custom-call | tf_op jit(solution)/shard_map/reduce_grads/pallas_call | solution.py:218
  (369 shorter events, 375.5 us)
Async XLA Ops:
  7.2 73.8 %copy-start = (bf16[960,960]{1,0:T(8,128)(2,1)S(1)}, bf16[960,960]{1,0:T(8,128)(2,1)}, u32[]{:S(2)}) copy-start(bf16[960,960]{1,0:T(8,128)(2,1)} %param.20) | copy-start | bytes 5529604
  7.2 33.0 %all-gather.7.cloned.1.call-start = ((), (), s32[]{:S(2)}) async-start(), calls=%async_computation.6 | async-start | bytes 2048000 | tf_op jit(solution)/shard_map/all_gather | solution.py:293
  9.3 20.0 %copy-start.63 = (f32[320]{0:T(512)}, f32[320]{0:T(512)S(1)}, u32[]{:S(2)}) copy-start(f32[320]{0:T(512)S(1)} %get-tuple-element.230) | copy-start | bytes 3844
  17.3 93.4 %all-gather.9.cloned.1.call-start = ((), (), s32[]{:S(2)}) async-start(), calls=%async_computation.7 | async-start | bytes 3276800 | tf_op jit(solution)/shard_map/all_gather | solution.py:303
  45.0 14.2 %copy-start.15 = (bf16[1,1280,320]{1,2,0:T(8,128)(2,1)}, bf16[1,1280,320]{1,2,0:T(8,128)(2,1)S(1)}, u32[]{:S(2)}) copy-start(bf16[1,1280,320]{1,2,0:T(8,128)(2,1)S(1)} %copy.131) | copy-start | bytes 2457604
  59.2 15.2 %copy-start.1 = (f32[5,3,320,1280]{3,2,1,0:T(8,128)S(1)}, f32[5,3,320,1280]{3,2,1,0:T(8,128)}, u32[]{:S(2)}) copy-start(f32[5,3,320,1280]{3,2,1,0:T(8,128)} %get-tuple-element.238) | copy-start | bytes 73728000
  83.3 93.9 %copy-start.5 = (f32[1,320,960]{2,1,0:T(8,128)}, f32[1,320,960]{2,1,0:T(8,128)S(1)}, u32[]{:S(2)}) copy-start(f32[1,320,960]{2,1,0:T(8,128)S(1)} %get-tuple-element.240) | copy-start | bytes 3686404
  83.9 31.2 %copy-start.65 = (f32[320]{0:T(512)}, f32[320]{0:T(512)S(1)}, u32[]{:S(2)}) copy-start(f32[320]{0:T(512)S(1)} %get-tuple-element.232) | copy-start | bytes 3844
  85.0 90.5 %reduce-scatter.19.cloned.1.call-start = ((), (), s32[]{:S(2)}) async-start(), calls=%async_computation.12 | async-start | bytes 3276800
  140.6 62.7 %all-gather.11.cloned.1.call-start = ((), (), s32[]{:S(2)}) async-start(), calls=%async_computation.8 | async-start | bytes 2048000 | tf_op jit(solution)/shard_map/all_gather | solution.py:293
  183.1 90.3 %all-gather.13.cloned.1.call-start = ((), (), s32[]{:S(2)}) async-start(), calls=%async_computation.9 | async-start | bytes 3276800 | tf_op jit(solution)/shard_map/all_gather | solution.py:303
  208.1 14.3 %copy-start.17 = (bf16[1,1280,320]{1,2,0:T(8,128)(2,1)}, bf16[1,1280,320]{1,2,0:T(8,128)(2,1)S(1)}, u32[]{:S(2)}) copy-start(bf16[1,1280,320]{1,2,0:T(8,128)(2,1)S(1)} %copy.136) | copy-start | bytes 2457604
  222.4 15.1 %copy-start.2 = (f32[5,3,320,1280]{3,2,1,0:T(8,128)S(1)}, f32[5,3,320,1280]{3,2,1,0:T(8,128)}, u32[]{:S(2)}) copy-start(f32[5,3,320,1280]{3,2,1,0:T(8,128)} %get-tuple-element.244) | copy-start | bytes 73728000
  247.7 52.8 %all-gather.15.cloned.1.call-start = ((), (), s32[]{:S(2)}) async-start(), calls=%async_computation.10 | async-start | bytes 3276800 | tf_op jit(solution)/shard_map/all_gather | solution.py:361
  248.3 118.0 %reduce-scatter.23.cloned.1.call-start = ((), (), s32[]{:S(2)}) async-start(), calls=%async_computation.14 | async-start | bytes 3276800
  331.5 72.1 %reduce-scatter.21.cloned.1.call-start = ((), (), s32[]{:S(2)}) async-start(), calls=%async_computation.13 | async-start | bytes 3276800
  354.2 148.3 %reduce-scatter.25.cloned.1.call-start = ((), (), s32[]{:S(2)}) async-start(), calls=%async_computation.15 | async-start | bytes 2048000
  440.6 16.4 %copy-start.35 = (bf16[1,320,15,32]{1,3,2,0:T(8,128)(2,1)S(1)}, bf16[1,320,15,32]{1,3,2,0:T(8,128)(2,1)}, u32[]{:S(2)}) copy-start(bf16[1,320,15,32]{1,3,2,0:T(8,128)(2,1)} %get-tuple-element.199) | copy-start | bytes 921604
  440.6 16.4 %copy-start.36 = (bf16[1,320,15,32]{1,3,2,0:T(8,128)(2,1)S(1)}, bf16[1,320,15,32]{1,3,2,0:T(8,128)(2,1)}, u32[]{:S(2)}) copy-start(bf16[1,320,15,32]{1,3,2,0:T(8,128)(2,1)} %get-tuple-element.200) | copy-start | bytes 921604
  473.8 70.6 %all-gather.17.cloned.1.call-start = ((), (), s32[]{:S(2)}) async-start(), calls=%async_computation.11 | async-start | bytes 3276800 | tf_op jit(solution)/shard_map/all_gather | solution.py:361
  518.6 90.0 %reduce-scatter.27.cloned.1.call-start = ((), (), s32[]{:S(2)}) async-start(), calls=%async_computation.16 | async-start | bytes 3276800
  573.8 134.0 %reduce-scatter.29.cloned.1.call-start = ((), (), s32[]{:S(2)}) async-start(), calls=%async_computation.17 | async-start | bytes 2048000
  645.9 16.4 %copy-start.33 = (bf16[1,320,15,32]{1,3,2,0:T(8,128)(2,1)S(1)}, bf16[1,320,15,32]{1,3,2,0:T(8,128)(2,1)}, u32[]{:S(2)}) copy-start(bf16[1,320,15,32]{1,3,2,0:T(8,128)(2,1)} %get-tuple-element.201) | copy-start | bytes 921604
  645.9 16.4 %copy-start.34 = (bf16[1,320,15,32]{1,3,2,0:T(8,128)(2,1)S(1)}, bf16[1,320,15,32]{1,3,2,0:T(8,128)(2,1)}, u32[]{:S(2)}) copy-start(bf16[1,320,15,32]{1,3,2,0:T(8,128)(2,1)} %get-tuple-element.202) | copy-start | bytes 921604
  (84 other events, 318.5 us)
Sparse Core Ops, SparseCore 0:
  17.4 22.7 all-gather.6
  85.1 25.5 all-gather.8
  140.7 34.6 reduce-scatter.18
  183.2 20.0 all-gather.10
  247.8 25.5 all-gather.12
  274.9 25.5 all-gather.14
  331.6 34.6 reduce-scatter.22
  368.8 34.6 reduce-scatter.20
  473.9 28.5 reduce-scatter.24
  518.7 25.5 all-gather.16
  573.9 34.6 reduce-scatter.26
  679.2 28.5 reduce-scatter.28

commit v2 on v1

v2 whole, which is shorter than its diff:
```python
import functools

import jax
import jax.numpy as jnp
from jax import lax
from jax.experimental import pallas as pl
from jax.experimental.pallas import tpu as pltpu
from jax.sharding import PartitionSpec as P

MESH_ID = pl.DeviceIdType.MESH
HEADS = 15
KV_HEADS = 5
GROUP = 3
HEAD_DIM = 64
EPSILON = 1e-05
THETA = 10000.0
CHUNKS = 2
MASKED = -1e30
LOW = jnp.bfloat16
FULL = jnp.float32
SCALE = HEAD_DIM ** (-0.5)
NT = (((1,), (1,)), ((), ()))
TN = (((0,), (0,)), ((), ()))


def device(seq_pos, dp_pos):
    return {"seq": seq_pos, "dp": dp_pos}


def send(src, dst, send_sem, recv_sem, target):
    copy = pltpu.make_async_remote_copy(
        src_ref=src,
        dst_ref=dst,
        send_sem=send_sem,
        recv_sem=recv_sem,
        device_id=target,
        device_id_type=MESH_ID,
    )
    copy.start()
    return copy


def greet(targets):
    barrier = pltpu.get_barrier_semaphore()
    for target in targets:
        pl.semaphore_signal(barrier, inc=1, device_id=target, device_id_type=MESH_ID)
    pl.semaphore_wait(barrier, len(targets))


def dot(left, right, dims=None):
    if dims is None:
        return jnp.dot(left, right, preferred_element_type=FULL)
    return lax.dot_general(left, right, dims, preferred_element_type=FULL)


def inverse_rms(value):
    return lax.rsqrt(jnp.mean(value * value, axis=-1, keepdims=True) + EPSILON)


def swap_halves(value):
    lane = lax.broadcasted_iota(jnp.int32, value.shape, 1)
    first = lax.rem(lane, HEAD_DIM) < HEAD_DIM // 2
    return jnp.where(first, pltpu.roll(value, 96, 1), pltpu.roll(value, 32, 1))


def attn_forward_kernel(
    res_ref, gains_ref, w_kvq_ref, w_out_ref, trig_ref, place_ref,
    normed_out, q_out, kv_out, log_out, mixed_out, after_out, normed_two_out,
    peak, total, acc, send_sem, recv_sem,
):
    seq, dp = lax.axis_index("seq"), lax.axis_index("dp")
    core, chip_x = lax.rem(seq, 2), lax.div(seq, 2)
    mate_seq, far_seq = seq + 1 - 2 * core, lax.rem(seq + 2, 4)
    mate, x_mate = device(mate_seq, dp), device(far_seq, dp)
    length = res_ref.shape[0]
    stacked = GROUP * length
    residual = res_ref[...]
    normed_out[...] = (residual * inverse_rms(residual) * gains_ref[0:1, :]).astype(LOW)
    kv_width = 2 * KV_HEADS * HEAD_DIM
    kv_pre = dot(normed_out[...], w_kvq_ref[:, :kv_width])
    for g in range(KV_HEADS):
        part = kv_pre[:, g * 128 : (g + 1) * 128]
        turned = part * trig_ref[2] + swap_halves(part) * trig_ref[3]
        kv_out[seq, :, g * 128 : (g + 1) * 128] = turned.astype(LOW)
    greet([mate, x_mate])
    own_kv = kv_out.at[seq]
    to_mate = send(own_kv, own_kv, send_sem.at[0], recv_sem.at[0], mate)
    to_x = send(own_kv, own_kv, send_sem.at[1], recv_sem.at[1], x_mate)
    q_pre = dot(normed_out[...], w_kvq_ref[:, kv_width:])
    lane = lax.broadcasted_iota(jnp.int32, (length, 128), 1)
    for pair in range((HEADS + 1) // 2):
        width = min(128, HEADS * HEAD_DIM - pair * 128)
        part = q_pre[:, pair * 128 : pair * 128 + width]
        if width < 128:
            part = jnp.concatenate([part, part], axis=1)
        turned = (part * trig_ref[0] + swap_halves(part) * trig_ref[1]) * SCALE
        q_out[2 * pair] = jnp.where(lane < HEAD_DIM, turned, 0.0).astype(LOW)
        if width == 128:
            q_out[2 * pair + 1] = jnp.where(lane < HEAD_DIM, pltpu.roll(turned, 64, 1), 0.0).astype(LOW)

    start, place = place_ref[0:1, :], place_ref[1:2, :]

    def attend(block, g, first):
        kv_g = kv_out[block, :, pl.ds(pl.multiple_of(g * 128, 128), 128)]
        q_g = q_out[pl.ds(3 * g, 3)].reshape(stacked, 128)
        scores = dot(kv_g, q_g, NT)
        key = lax.broadcasted_iota(jnp.int32, (length, stacked), 0) + block * length
        allowed = key >= start
        if first:
            allowed = allowed & (key <= place)
        scores = jnp.where(allowed, scores, MASKED)
        here = jnp.max(scores, axis=0, keepdims=True)
        if first:
            new_peak = here
        else:
            new_peak = jnp.maximum(peak[g], here)
        weights = jnp.exp(scores - new_peak)
        row_total = jnp.sum(weights, axis=0, keepdims=True)
        mix = dot(kv_g, weights.astype(LOW), TN)[HEAD_DIM:]
        if not first:
            fade = jnp.exp(peak[g] - new_peak)
            row_total = row_total + fade * total[g]
            mix = mix + fade * acc[g]
        peak[g], total[g], acc[g] = new_peak, row_total, mix

    @pl.loop(0, KV_HEADS)
    def _(g):
        attend(seq, g, True)

    to_mate.wait()

    @pl.when(core == 1)
    def _():
        @pl.loop(0, KV_HEADS)
        def _(g):
            attend(mate_seq, g, False)

    to_x.wait()
    far_kv = kv_out.at[far_seq]
    onward = send(far_kv, far_kv, send_sem.at[2], recv_sem.at[2], mate)

    @pl.when(chip_x == 1)
    def _():
        @pl.loop(0, KV_HEADS)
        def _(g):
            attend(far_seq, g, False)

    onward.wait()

    @pl.when(chip_x == 1)
    def _():
        @pl.loop(0, KV_HEADS)
        def _(g):
            attend(lax.rem(mate_seq + 2, 4), g, False)

    for g in range(KV_HEADS):
        heads = (acc[g] / total[g]).T.astype(LOW)
        log_out[g] = peak[g] + jnp.log(total[g])
        for i in range(GROUP):
            h = GROUP * g + i
            mixed_out[:, h * HEAD_DIM : (h + 1) * HEAD_DIM] = heads[i * length : (i + 1) * length]
    after = residual + dot(mixed_out[...], w_out_ref[...])
    after_out[...] = after
    normed_two_out[...] = (after * inverse_rms(after) * gains_ref[1:2, :]).astype(LOW)


VMEM = pl.BlockSpec(memory_space=pltpu.VMEM)


def attn_forward(residual, gains, w_kvq, w_out, trig, place):
    length, width = residual.shape
    kv_width = 2 * KV_HEADS * HEAD_DIM
    shapes = (
        ((length, width), LOW),
        ((HEADS, length, 128), LOW),
        ((4, length, kv_width), LOW),
        ((KV_HEADS, 1, GROUP * length), FULL),
        ((length, HEADS * HEAD_DIM), LOW),
        ((length, width), FULL),
        ((length, width), LOW),
    )
    return pl.pallas_call(
        attn_forward_kernel,
        out_shape=tuple(jax.ShapeDtypeStruct(*s) for s in shapes),
        in_specs=[VMEM] * 6,
        out_specs=(VMEM,) * len(shapes),
        scratch_shapes=[
            pltpu.VMEM((KV_HEADS, 1, GROUP * length), FULL),
            pltpu.VMEM((KV_HEADS, 1, GROUP * length), FULL),
            pltpu.VMEM((KV_HEADS, HEAD_DIM, GROUP * length), FULL),
            pltpu.SemaphoreType.DMA((3,)),
            pltpu.SemaphoreType.DMA((3,)),
        ],
        compiler_params=pltpu.CompilerParams(
            collective_id=1, has_side_effects=True, vmem_limit_bytes=60 * 1024 * 1024
        ),
        name="attn_forward",
    )(residual, gains, w_kvq, w_out, trig, place)


def prepare(positions, w_query, w_key, w_value):
    length = positions.shape[0]
    frequency = THETA ** (-(jnp.arange(HEAD_DIM // 2, dtype=FULL) * 2.0 / HEAD_DIM))
    angles = positions.astype(FULL)[:, None] * frequency
    cos, sin = jnp.cos(angles), jnp.sin(angles)
    one, none = jnp.ones((length, HEAD_DIM), FULL), jnp.zeros((length, HEAD_DIM), FULL)
    trig = jnp.stack(
        [
            jnp.concatenate([cos, cos, cos, cos], 1),
            jnp.concatenate([-sin, sin, -sin, sin], 1),
            jnp.concatenate([cos, cos, one], 1),
            jnp.concatenate([-sin, sin, none], 1),
        ]
    )
    width = w_key.shape[0]
    pairs = jnp.stack([w_key.reshape(width, KV_HEADS, HEAD_DIM), w_value.reshape(width, KV_HEADS, HEAD_DIM)], axis=2)
    w_kvq = jnp.concatenate([pairs.reshape(width, -1), w_query], axis=1)
    own = lax.axis_index("seq") * length + jnp.arange(length, dtype=jnp.int32)
    place = jnp.stack([jnp.tile(own - positions, GROUP), jnp.tile(own, GROUP)])
    place = jnp.pad(place, ((0, 6), (0, 0)))
    return trig, w_kvq, place


def ffn_forward_kernel(
    after_ref, normed_ref, w_gate_ref, w_up_ref, w_down_ref,
    res_out, rows_out, gate_out, up_out,
    mate_send, mate_recv, x_send, x_recv, own_far,
    send_sem, recv_sem,
):
    seq, dp = lax.axis_index("seq"), lax.axis_index("dp")
    core = lax.rem(seq, 2)
    mate_seq, far_seq = seq + 1 - 2 * core, lax.rem(seq + 2, 4)
    far_mate = lax.rem(mate_seq + 2, 4)
    mate, x_mate = device(mate_seq, dp), device(far_seq, dp)
    length = after_ref.shape[0]
    step = length // CHUNKS
    greet([mate, x_mate])
    part = lambda k: pl.ds(k * step, step)

    def hop(index, src, dst, target):
        return send(src, dst, send_sem.at[index], recv_sem.at[index], target)

    rows_out[seq] = normed_ref[...]
    own_rows = lambda k: rows_out.at[seq, part(k)]
    far_rows = lambda k: rows_out.at[far_seq, part(k)]
    to_x = [hop(k, own_rows(k), own_rows(k), x_mate) for k in range(CHUNKS)]
    to_mate = hop(CHUNKS, rows_out.at[seq], rows_out.at[seq], mate)
    base = CHUNKS + 1

    def ffn(quarter, rows):
        block = rows_out[quarter, rows]
        gate = dot(block, w_gate_ref[...])
        up = dot(block, w_up_ref[...])
        gate_out[quarter, rows] = gate.astype(LOW)
        up_out[quarter, rows] = up.astype(LOW)
        hidden = (gate * jax.nn.sigmoid(gate) * up).astype(LOW)
        return dot(hidden, w_down_ref[...])

    everything = pl.ds(0, length)
    res_out[...] = after_ref[...] + ffn(seq, everything)
    to_mate.wait()
    mate_send[0] = ffn(mate_seq, everything).astype(LOW)
    back = hop(base, mate_send.at[0], mate_recv.at[0], mate)
    onward = []
    for k in range(CHUNKS):
        to_x[k].wait()
        onward.append(hop(base + 1 + k, far_rows(k), far_rows(k), mate))
        own_far[part(k)] = ffn(far_seq, part(k))
        onward[k].wait()
        mate_send[1, part(k)] = ffn(far_mate, part(k)).astype(LOW)
        joint = hop(base + 1 + CHUNKS + k, mate_send.at[1, part(k)], mate_recv.at[1, part(k)], mate)
        joint.wait()
        x_send[part(k)] = (own_far[part(k)] + mate_recv[1, part(k)].astype(FULL)).astype(LOW)
        onward.append(
            hop(base + 1 + 2 * CHUNKS + k, x_send.at[part(k)], x_recv.at[part(k)], x_mate)
        )
        onward[k], onward[-1] = onward[-1], onward[k]
        onward.pop()
    back.wait()
    res_out[...] += mate_recv[0].astype(FULL)
    for k in range(CHUNKS):
        onward[k].wait()
        res_out[part(k)] += x_recv[part(k)].astype(FULL)


def ffn_forward(after, normed_two, w_gate, w_up, w_down):
    length, width = after.shape
    hidden = w_gate.shape[1]
    shapes = (
        ((length, width), FULL),
        ((4, length, width), LOW),
        ((4, length, hidden), LOW),
        ((4, length, hidden), LOW),
    )
    sems = 3 * CHUNKS + CHUNKS + 2
    return pl.pallas_call(
        ffn_forward_kernel,
        out_shape=tuple(jax.ShapeDtypeStruct(*s) for s in shapes),
        in_specs=[VMEM] * 5,
        out_specs=(VMEM,) * len(shapes),
        scratch_shapes=[
            pltpu.VMEM((2, length, width), LOW),
            pltpu.VMEM((2, length, width), LOW),
            pltpu.VMEM((length, width), LOW),
            pltpu.VMEM((length, width), LOW),
            pltpu.VMEM((length, width), FULL),
            pltpu.SemaphoreType.DMA((sems,)),
            pltpu.SemaphoreType.DMA((sems,)),
        ],
        compiler_params=pltpu.CompilerParams(
            collective_id=2, has_side_effects=True, vmem_limit_bytes=60 * 1024 * 1024
        ),
        name="ffn_forward",
    )(after, normed_two, w_gate, w_up, w_down)


def norm_back(value, gain, grad):
    inverse = inverse_rms(value)
    weighted = grad * gain
    inner = jnp.mean(weighted * value, axis=-1, keepdims=True)
    back = inverse * weighted - value * (inverse * inverse * inverse) * inner
    return back, jnp.sum(grad * value * inverse, axis=0, keepdims=True)


def ffn_backward_kernel(
    up_ref, after_ref, gains_ref, rows_ref, gate_ref, upp_ref, w_gate_ref, w_up_ref, w_down_ref, *rest
):
    (prev_ref,) = rest[:-14] if len(rest) == 15 else (None,)
    (
        grad_out, gain_out, weight_out,
        low_all, gate_grad, up_grad, hidden,
        mate_send, mate_recv, x_send, x_recv, own_far,
        send_sem, recv_sem,
    ) = rest[-14:]
    seq, dp = lax.axis_index("seq"), lax.axis_index("dp")
    core, chip_x = lax.rem(seq, 2), lax.div(seq, 2)
    mate_seq, far_seq = seq + 1 - 2 * core, lax.rem(seq + 2, 4)
    far_mate = lax.rem(mate_seq + 2, 4)
    mate, x_mate = device(mate_seq, dp), device(far_seq, dp)
    length, width = up_ref.shape
    step = length // CHUNKS
    greet([mate, x_mate])
    part = lambda k: pl.ds(k * step, step)

    def hop(index, src, dst, target):
        return send(src, dst, send_sem.at[index], recv_sem.at[index], target)

    low_all[seq] = up_ref[...].astype(LOW)
    own_rows = lambda k: low_all.at[seq, part(k)]
    far_rows = lambda k: low_all.at[far_seq, part(k)]
    to_x = [hop(k, own_rows(k), own_rows(k), x_mate) for k in range(CHUNKS)]
    to_mate = hop(CHUNKS, low_all.at[seq], low_all.at[seq], mate)
    base = CHUNKS + 1

    def ffn(quarter, rows):
        hidden_grad = dot(low_all[quarter, rows], w_down_ref[...], NT)
        gate = gate_ref[quarter, rows].astype(FULL)
        up = upp_ref[quarter, rows].astype(FULL)
        bend = jax.nn.sigmoid(gate)
        silu = gate * bend
        hidden[quarter, rows] = (silu * up).astype(LOW)
        gate_low = (hidden_grad * up * bend * (1.0 + gate * (1.0 - bend))).astype(LOW)
        up_low = (hidden_grad * silu).astype(LOW)
        gate_grad[quarter, rows] = gate_low
        up_grad[quarter, rows] = up_low
        return dot(gate_low, w_gate_ref[...], NT) + dot(up_low, w_up_ref[...], NT)

    def weights(first_quarter, first):
        pair = lambda ref: ref[pl.ds(first_quarter, 2)].reshape(2 * length, ref.shape[2])
        rows, low = pair(rows_ref), pair(low_all)
        for i, (left, right) in enumerate(
            ((rows, pair(gate_grad)), (rows, pair(up_grad)), (low, pair(hidden)))
        ):
            term = dot(left, right, TN)
            if not first:
                term = term + weight_out[i]
            elif prev_ref is not None:
                term = term + prev_ref[i]
            weight_out[i] = term

    everything = pl.ds(0, length)
    grad_out[...] = ffn(seq, everything)
    to_mate.wait()
    mate_send[0] = ffn(mate_seq, everything).astype(LOW)
    back = hop(base, mate_send.at[0], mate_recv.at[0], mate)
    last = []
    for k in range(CHUNKS):
        to_x[k].wait()
        onward = hop(base + 1 + k, far_rows(k), far_rows(k), mate)
        own_far[part(k)] = ffn(far_seq, part(k))
        onward.wait()
        mate_send[1, part(k)] = ffn(far_mate, part(k)).astype(LOW)
        joint = hop(base + 1 + CHUNKS + k, mate_send.at[1, part(k)], mate_recv.at[1, part(k)], mate)
        joint.wait()
        x_send[part(k)] = (own_far[part(k)] + mate_recv[1, part(k)].astype(FULL)).astype(LOW)
        last.append(hop(base + 1 + 2 * CHUNKS + k, x_send.at[part(k)], x_recv.at[part(k)], x_mate))
        if k == 0:
            weights(2 * chip_x, True)
    weights(2 - 2 * chip_x, False)
    back.wait()
    total = grad_out[...] + mate_recv[0].astype(FULL)
    for k in range(CHUNKS):
        last[k].wait()
    total = total + x_recv[...].astype(FULL)
    sent_back, gain_term = norm_back(after_ref[...], gains_ref[1:2, :], total)
    grad_out[...] = up_ref[...] + sent_back
    gain_out[...] = jnp.broadcast_to(gain_term, gain_out.shape)


def ffn_backward(upstream, after, gains, rows_all, gate_all, up_all, w_gate, w_up, w_down, prev=None):
    length, width = after.shape
    hidden = w_gate.shape[1]
    shapes = (
        ((length, width), FULL),
        ((8, width), FULL),
        ((3, width, hidden), FULL),
    )
    sems = 3 * CHUNKS + CHUNKS + 2
    args = (upstream, after, gains, rows_all, gate_all, up_all, w_gate, w_up, w_down)
    if prev is not None:
        args = args + (prev,)
    return pl.pallas_call(
        ffn_backward_kernel,
        out_shape=tuple(jax.ShapeDtypeStruct(*s) for s in shapes),
        in_specs=[VMEM] * len(args),
        out_specs=(VMEM,) * len(shapes),
        scratch_shapes=[
            pltpu.VMEM((4, length, width), LOW),
            pltpu.VMEM((4, length, hidden), LOW),
            pltpu.VMEM((4, length, hidden), LOW),
            pltpu.VMEM((4, length, hidden), LOW),
            pltpu.VMEM((2, length, width), LOW),
            pltpu.VMEM((2, length, width), LOW),
            pltpu.VMEM((length, width), LOW),
            pltpu.VMEM((length, width), LOW),
            pltpu.VMEM((length, width), FULL),
            pltpu.SemaphoreType.DMA((sems,)),
            pltpu.SemaphoreType.DMA((sems,)),
        ],
        compiler_params=pltpu.CompilerParams(
            collective_id=3 if prev is None else 4, has_side_effects=True, vmem_limit_bytes=60 * 1024 * 1024
        ),
        name="ffn_backward",
    )(*args)


def attn_backward_kernel(
    after_grad_ref, res_ref, normed_ref, gains_ref, q_ref, kv_ref, log_ref, mixed_ref,
    w_kvq_ref, w_out_ref, trig_ref, place_ref, *rest
):
    (prev_ref,) = rest[:-12] if len(rest) == 13 else (None,)
    (
        grad_out, gain_out, weight_out,
        mixed_grad, delta, kv_grad, query_grad, back,
        grad_send, grad_recv,
        send_sem, recv_sem,
    ) = rest[-12:]
    seq, dp = lax.axis_index("seq"), lax.axis_index("dp")
    core, chip_x = lax.rem(seq, 2), lax.div(seq, 2)
    mate_seq, far_seq = seq + 1 - 2 * core, lax.rem(seq + 2, 4)
    far_mate = lax.rem(mate_seq + 2, 4)
    mate, x_mate = device(mate_seq, dp), device(far_seq, dp)
    length, width = res_ref.shape
    stacked = GROUP * length
    kv_width = 2 * KV_HEADS * HEAD_DIM
    greet([mate, x_mate])

    def hop(index, src, dst, target):
        return send(src, dst, send_sem.at[index], recv_sem.at[index], target)

    low_grad = after_grad_ref[...].astype(LOW)
    mixed_back = dot(low_grad, w_out_ref[...], NT)
    lane = lax.broadcasted_iota(jnp.int32, (length, 128), 1)
    for pair in range((HEADS + 1) // 2):
        span = min(128, HEADS * HEAD_DIM - pair * 128)
        part = mixed_back[:, pair * 128 : pair * 128 + span]
        if span < 128:
            part = jnp.concatenate([part, part], axis=1)
        else:
            mixed_grad[2 * pair + 1] = jnp.where(lane >= HEAD_DIM, part, 0.0).astype(LOW)
        mixed_grad[2 * pair] = jnp.where(lane >= HEAD_DIM, pltpu.roll(part, 64, 1), 0.0).astype(LOW)
    product = mixed_back.astype(LOW).astype(FULL) * mixed_ref[...].astype(FULL)
    high = product.astype(LOW)
    rest_low = (product - high.astype(FULL)).astype(LOW)
    head = lax.broadcasted_iota(jnp.int32, (16, HEADS * HEAD_DIM), 0)
    column = lax.broadcasted_iota(jnp.int32, (16, HEADS * HEAD_DIM), 1)
    pick = jnp.where(lax.div(column, HEAD_DIM) == head, 1.0, 0.0).astype(LOW)
    sums = dot(pick, high, NT) + dot(pick, rest_low, NT)
    for g in range(KV_HEADS):
        delta[g] = jnp.concatenate([sums[3 * g + i : 3 * g + i + 1] for i in range(GROUP)], axis=1)
    query_grad[...] = jnp.zeros_like(query_grad)

    start, place = place_ref[0:1, :], place_ref[1:2, :]

    def attend(block, g, diagonal):
        columns = pl.ds(pl.multiple_of(g * 128, 128), 128)
        kv_g = kv_ref[block, :, columns]
        q_g = q_ref[pl.ds(3 * g, 3)].reshape(stacked, 128)
        out_g = mixed_grad[pl.ds(3 * g, 3)].reshape(stacked, 128)
        scores = dot(kv_g, q_g, NT)
        key = lax.broadcasted_iota(jnp.int32, (length, stacked), 0) + block * length
        allowed = key >= start
        if diagonal:
            allowed = allowed & (key <= place)
        weights = jnp.where(allowed, jnp.exp(scores - log_ref[g]), 0.0)
        probs_grad = dot(kv_g, out_g, NT)
        score_grad = (weights * (probs_grad - delta[g])).astype(LOW)
        kv_grad[block, :, columns] = dot(weights.astype(LOW), out_g) + dot(score_grad, q_g)
        query_grad[g] += dot(kv_g, score_grad, TN)[:HEAD_DIM]

    def attend_all(block, condition, diagonal=False):
        @pl.when(condition)
        def _():
            @pl.loop(0, KV_HEADS)
            def _(g):
                attend(block, g, diagonal)

        if not diagonal:
            @pl.when(jnp.logical_not(condition))
            def _():
                kv_grad[block] = jnp.zeros_like(kv_grad[block])

    right = chip_x == 1
    attend_all(far_mate, right)
    grad_send[0] = kv_grad[far_mate].astype(LOW)
    joint = hop(0, grad_send.at[0], grad_recv.at[0], mate)
    attend_all(far_seq, right)
    joint.wait()
    grad_send[1] = (kv_grad[far_seq] + grad_recv[0].astype(FULL)).astype(LOW)
    across = hop(1, grad_send.at[1], grad_recv.at[1], x_mate)
    attend_all(mate_seq, core == 1)
    grad_send[2] = kv_grad[mate_seq].astype(LOW)
    beside = hop(2, grad_send.at[2], grad_recv.at[2], mate)
    attend_all(seq, seq >= 0, True)

    for g in range(KV_HEADS):
        heads = query_grad[g].T * SCALE
        for i in range(GROUP):
            h = GROUP * g + i
            part = heads[i * length : (i + 1) * length]
            part = jnp.concatenate([part, part], axis=1)
            turned = part * trig_ref[0] - swap_halves(part) * trig_ref[1]
            at = kv_width + h * HEAD_DIM
            back[:, at : at + HEAD_DIM] = turned[:, :HEAD_DIM].astype(LOW)

    def weight(block, at, left, right):
        columns = slice(at, at + right.shape[1])
        term = dot(left, right, TN)
        weight_out[block, :, columns] = term if prev_ref is None else term + prev_ref[block, :, columns]

    third = width // 3
    cut = kv_width + 2 * third
    weight(2, 0, mixed_ref[...], low_grad[:, : 2 * third])
    weight(3, third, mixed_ref[...], low_grad[:, 2 * third :])
    weight(1, 0, normed_ref[...], back[:, kv_width:cut])
    weight(3, 0, normed_ref[...], back[:, cut:])
    normed_grad = dot(back[:, kv_width:], w_kvq_ref[:, kv_width:], NT)

    across.wait()
    beside.wait()
    own = kv_grad[seq] + grad_recv[1].astype(FULL) + grad_recv[2].astype(FULL)
    for g in range(KV_HEADS):
        part = own[:, g * 128 : (g + 1) * 128]
        back[:, g * 128 : (g + 1) * 128] = (part * trig_ref[2] - swap_halves(part) * trig_ref[3]).astype(LOW)
    weight(0, 0, normed_ref[...], back[:, :kv_width])
    normed_grad = normed_grad + dot(back[:, :kv_width], w_kvq_ref[:, :kv_width], NT)
    sent_back, gain_term = norm_back(res_ref[...], gains_ref[0:1, :], normed_grad)
    grad_out[...] = after_grad_ref[...] + sent_back
    gain_out[...] = jnp.broadcast_to(gain_term, gain_out.shape)


def attn_backward(
    after_grad, residual, normed, gains, q, kv, log_total, mixed, w_kvq, w_out, trig, place, prev=None
):
    length, width = residual.shape
    kv_width = 2 * KV_HEADS * HEAD_DIM
    args = (after_grad, residual, normed, gains, q, kv, log_total, mixed, w_kvq, w_out, trig, place)
    if prev is not None:
        args = args + (prev,)
    shapes = (
        ((length, width), FULL),
        ((8, width), FULL),
        ((4, width, kv_width), FULL),
    )
    return pl.pallas_call(
        attn_backward_kernel,
        out_shape=tuple(jax.ShapeDtypeStruct(*s) for s in shapes),
        in_specs=[VMEM] * len(args),
        out_specs=(VMEM,) * len(shapes),
        scratch_shapes=[
            pltpu.VMEM((HEADS, length, 128), LOW),
            pltpu.VMEM((KV_HEADS, 1, GROUP * length), FULL),
            pltpu.VMEM((4, length, kv_width), FULL),
            pltpu.VMEM((KV_HEADS, HEAD_DIM, GROUP * length), FULL),
            pltpu.VMEM((length, kv_width + width), LOW),
            pltpu.VMEM((3, length, kv_width), LOW),
            pltpu.VMEM((3, length, kv_width), LOW),
            pltpu.SemaphoreType.DMA((3,)),
            pltpu.SemaphoreType.DMA((3,)),
        ],
        compiler_params=pltpu.CompilerParams(
            collective_id=5 if prev is None else 6, has_side_effects=True, vmem_limit_bytes=60 * 1024 * 1024
        ),
        name="attn_backward",
    )(*args)


def reduce_kernel(
    attn_ref, ffn_ref, gain_ref,
    attn_out, ffn_out, gain_out,
    core_send, core_recv, x_send, x_recv, own,
    y_send, y_recv, z_send, z_recv, g_recv, share_low,
    send_sem, recv_sem,
):
    seq, dp = lax.axis_index("seq"), lax.axis_index("dp")
    core, chip_x = lax.rem(seq, 2), lax.div(seq, 2)
    row_y, row_z = lax.rem(dp, 2), lax.div(dp, 2)
    mate = device(seq + 1 - 2 * core, dp)
    x_mate = device(lax.rem(seq + 2, 4), dp)
    y_mate = device(seq, dp + 1 - 2 * row_y)
    z_of = [lax.rem(row_z + k, 4) for k in range(1, 4)]
    z_mates = [device(seq, z * 2 + row_y) for z in z_of]
    greet([mate, x_mate, y_mate] + z_mates)
    low = jnp.bfloat16

    def y_start(index, load):
        for z in range(4):
            y_send[index, z] = load(2 * z + 1 - row_y).astype(low)
        return send(y_send.at[index], y_recv.at[index], send_sem.at[index], recv_sem.at[index], y_mate)

    def z_start(index, load):
        copies = []
        for k in range(3):
            z = z_of[k]
            z_send[index, k] = (load(2 * z + row_y) + y_recv[index, z].astype(jnp.float32)).astype(low)
            sem = 4 + 3 * index + k
            copies.append(
                send(z_send.at[index, k], z_recv.at[index, k], send_sem.at[sem], recv_sem.at[sem], z_mates[k])
            )
        return copies

    def z_finish(index, load, copies):
        total = load(2 * row_z + row_y) + y_recv[index, row_z].astype(jnp.float32)
        for k in range(3):
            copies[k].wait()
            total = total + z_recv[index, k].astype(jnp.float32)
        return total

    gain_out[...] = gain_ref[...]
    hops = [mate, x_mate, y_mate, device(seq, lax.rem(dp + 4, 8)), device(seq, dp + 2 - 4 * lax.rem(row_z, 2))]

    def gain_start(hop):
        sem = 22 + hop
        return send(gain_ref if hop == 0 else gain_out, g_recv.at[hop], send_sem.at[sem], recv_sem.at[sem], hops[hop])

    for half in range(2):
        core_send[half] = attn_ref[2 * half + 1 - core].astype(low)
    core_copy = send(core_send, core_recv, send_sem.at[16], recv_sem.at[16], mate)
    gain_copy = gain_start(0)
    ffn_load = lambda m: (lambda j: ffn_ref[m, j])
    y_copies = [y_start(m, ffn_load(m)) for m in range(3)]
    core_copy.wait()
    x_send[...] = (
        attn_ref[2 * (1 - chip_x) + core] + core_recv[1 - chip_x].astype(jnp.float32)
    ).astype(low)
    x_copy = send(x_send, x_recv, send_sem.at[17], recv_sem.at[17], x_mate)
    own[...] = attn_ref[seq] + core_recv[chip_x].astype(jnp.float32)
    for hop in range(5):
        gain_copy.wait()
        gain_out[...] += g_recv[hop]
        if hop < 4:
            gain_copy = gain_start(hop + 1)
    z_copies = []
    for m in range(3):
        y_copies[m].wait()
        z_copies.append(z_start(m, ffn_load(m)))
    x_copy.wait()
    own[...] += x_recv[...].astype(jnp.float32)
    own_load = lambda j: own[j]
    y_copy = y_start(3, own_load)
    for m in range(3):
        ffn_out[m] = z_finish(m, ffn_load(m), z_copies[m])
    y_copy.wait()
    z_copy = z_start(3, own_load)
    share_low[seq] = z_finish(3, own_load, z_copy).astype(low)
    to_mate = send(share_low.at[seq], share_low.at[seq], send_sem.at[18], recv_sem.at[18], mate)
    to_x = send(share_low.at[seq], share_low.at[seq], send_sem.at[19], recv_sem.at[19], x_mate)
    to_x.wait()
    far = lax.rem(seq + 2, 4)
    onward = send(share_low.at[far], share_low.at[far], send_sem.at[20], recv_sem.at[20], mate)
    to_mate.wait()
    onward.wait()
    attn_out[...] = share_low[...].astype(jnp.float32)


def reduce_grads(attn_grads, ffn_grads, gain_grads):
    share, cols = attn_grads.shape[2:]
    low, full = jnp.bfloat16, jnp.float32
    vmem = pl.BlockSpec(memory_space=pltpu.VMEM)
    return pl.pallas_call(
        reduce_kernel,
        out_shape=(
            jax.ShapeDtypeStruct((4, share, cols), full),
            jax.ShapeDtypeStruct((3, share, cols), full),
            jax.ShapeDtypeStruct(gain_grads.shape, full),
        ),
        in_specs=[vmem] * 3,
        out_specs=(vmem, vmem, vmem),
        scratch_shapes=[
            pltpu.VMEM((2, 8, share, cols), low),
            pltpu.VMEM((2, 8, share, cols), low),
            pltpu.VMEM((8, share, cols), low),
            pltpu.VMEM((8, share, cols), low),
            pltpu.VMEM((8, share, cols), full),
            pltpu.VMEM((4, 4, share, cols), low),
            pltpu.VMEM((4, 4, share, cols), low),
            pltpu.VMEM((4, 3, share, cols), low),
            pltpu.VMEM((4, 3, share, cols), low),
            pltpu.VMEM((5,) + gain_grads.shape, full),
            pltpu.VMEM((4, share, cols), low),
            pltpu.SemaphoreType.DMA((27,)),
            pltpu.SemaphoreType.DMA((27,)),
        ],
        compiler_params=pltpu.CompilerParams(
            collective_id=0, has_side_effects=True, vmem_limit_bytes=60 * 1024 * 1024
        ),
        name="reduce_grads",
    )(attn_grads, ffn_grads, gain_grads)


def unpack(grads):
    rows, columns = grads.shape[1:]
    pairs = grads[0].reshape(rows, KV_HEADS, 2, HEAD_DIM)
    half = columns // 2
    return (
        jnp.concatenate([grads[1], grads[3][:, :half]], axis=1),
        pairs[:, :, 0].reshape(rows, -1),
        pairs[:, :, 1].reshape(rows, -1),
        jnp.concatenate([grads[2], grads[3][:, half:]], axis=1),
    )


def on_device(
    tokens,
    seg_ids,
    positions,
    attn_gain,
    w_query,
    w_key,
    w_value,
    w_out,
    ffn_gain,
    w_gate,
    w_up,
    w_down,
    cotangent,
):
    width = tokens.shape[2]
    trig, w_kvq, place = prepare(positions[0], w_query, w_key, w_value)
    gains = jnp.pad(jnp.stack([attn_gain, ffn_gain]), ((0, 6), (0, 0)))
    residual = tokens[0].astype(FULL)
    kept = []
    for repeat in range(2):
        normed, q, kv, log_total, mixed, after, normed_two = attn_forward(
            residual, gains, w_kvq, w_out, trig, place
        )
        result, rows_all, gate_all, up_all = ffn_forward(after, normed_two, w_gate, w_up, w_down)
        kept.append((residual, normed, q, kv, log_total, mixed, after, rows_all, gate_all, up_all))
        residual = result
    output = residual.astype(LOW)
    upstream = cotangent[0].astype(FULL)
    ffn_grads, attn_grads, gain_terms = None, None, []
    for repeat in (1, 0):
        residual, normed, q, kv, log_total, mixed, after, rows_all, gate_all, up_all = kept[repeat]
        after_grad, ffn_gain_term, ffn_grads = ffn_backward(
            upstream, after, gains, rows_all, gate_all, up_all, w_gate, w_up, w_down, ffn_grads
        )
        upstream, attn_gain_term, attn_grads = attn_backward(
            after_grad, residual, normed, gains, q, kv, log_total, mixed, w_kvq, w_out, trig, place, attn_grads
        )
        gain_terms.append(jnp.stack([attn_gain_term[0], ffn_gain_term[0]]))
    gain_grads = gain_terms[0] + gain_terms[1]
    if lax.axis_size("dp") == 8 and width % 64 == 0:
        share = width // 8
        own = gain_grads.reshape(2, 8, share).transpose(1, 0, 2)
        own = jnp.pad(own, ((0, 0), (0, 6), (0, 128 - share)))
        attn_share, ffn_share, gain_share = reduce_grads(
            attn_grads.reshape(4, 8, share, -1), ffn_grads.reshape(3, 8, share, -1), own
        )
        own_gains = lax.dynamic_index_in_dim(gain_share, lax.axis_index("dp"), 0, keepdims=False)[:2, :share]
    else:

        def over_rows(grads, dim):
            grads = lax.psum_scatter(grads.astype(LOW), "dp", scatter_dimension=dim, tiled=True)
            return grads.astype(FULL)

        def over_all(grads, dim):
            return lax.psum(over_rows(grads, dim).astype(LOW), "seq").astype(FULL)

        attn_share = over_all(attn_grads, 1)
        ffn_share = over_rows(ffn_grads, 1)
        own_gains = over_all(gain_grads, 1)
    query_share, key_share, value_share, out_share = unpack(attn_share)
    return (
        output[None],
        upstream[None],
        own_gains[0],
        query_share,
        key_share,
        value_share,
        out_share,
        own_gains[1],
        ffn_share[0],
        ffn_share[1],
        ffn_share[2].T,
    )


def solution(mesh):
    in_specs = (
        P("dp", "seq", None),
        P("dp", "seq"),
        P("dp", "seq"),
        P(),
        P(),
        P(),
        P(),
        P(),
        P(),
        P(None, "seq"),
        P(None, "seq"),
        P("seq", None),
        P("dp", "seq", None),
    )
    out_specs = (
        P("dp", "seq", None),
        P("dp", "seq", None),
        P("dp"),
        P("dp", None),
        P("dp", None),
        P("dp", None),
        P("dp", None),
        P("dp"),
        P("dp", "seq"),
        P("dp", "seq"),
        P("seq", "dp"),
    )
    return jax.shard_map(
        on_device, mesh=mesh, in_specs=in_specs, out_specs=out_specs, check_vma=False
    )
```

time: 915 us -> 459 us (0.50)
  Pallas kernels: 115 us -> 422 us
  matrix products: 243 us -> 0 us
  waiting for transfers between devices: 226 us -> 0 us
  local copies, waits for them, and re-layouts: 206 us -> 15.1 us
  other arithmetic: 87.1 us -> 13.2 us
  between operations: 16.3 us -> 1.08 us
    pallas_call x0 -> x8, Pallas kernels: none -> 299 us  [the longest x2 90.4 us: ffn_backward(): pl.pallas_call(ffn_backward_kernel, out_shape=tuple((jax.ShapeDtypeStruct...]
    dot_general x54 -> x0, matrix products: 243 us -> none  [the longest x2 39.4 us: row_backward(): jnp.einsum('qkgd,tkd->kgqt', mixed_grad, values_all, preferred_element_ty...]
    unnamed x220 -> x18, local copies, waits for them, and re-layouts: 137 us -> 4.41 us
    all_gather x6 -> x0, waiting for transfers between devices: 115 us -> none  [the longest x2 50.1 us: on_device(): normed_two = lax.all_gather(normed_two, 'seq', axis=1, tiled=True)]
    unnamed x18 -> x0, waiting for transfers between devices: 111 us -> none
    convert_element_type x11 -> x3, other arithmetic: 38.5 us -> 3.21 us  [the longest x1 1.3 us: on_device(): upstream = cotangent[0].astype(FULL)]
    reduce_sum x6 -> x0, other arithmetic: 26.3 us -> none  [the longest x2 22.7 us: row_attend(): row_total = jnp.sum(shifted, axis=-1, keepdims=True)]
    reshape x3 -> x1, local copies, waits for them, and re-layouts: 22 us -> 1.15 us  [prepare(): w_kvq = jnp.concatenate([pairs.reshape(width, -1), w_query], axis=1)]
  transfers between devices with their start and end apart: 12 -> 0, of which waited for: 12 -> 0; matrix products, arithmetic and copies ran while one was open for 12% -> 0% of each run, Pallas kernels for 0% -> 0%
where the time goes in v2:
time: 459 us; the launch traced here: 451 us
  Pallas kernels  422 us (92%)
  local copies, waits for them, and re-layouts  15.1 us (3%)
  other arithmetic  13.2 us (3%)
    pallas_call x1, Pallas kernels, reduce_grads(): pl.pallas_call(reduce_kernel, out_shape=(jax.ShapeDtypeStruct((4, share,...  123 us
    pallas_call x2, Pallas kernels, ffn_backward(): pl.pallas_call(ffn_backward_kernel, out_shape=tuple((jax.ShapeDtypeStruct...  90.4 us
    pallas_call x2, Pallas kernels, ffn_forward(): pl.pallas_call(ffn_forward_kernel, out_shape=tuple((jax.ShapeDtypeStruct(...  88.1 us
    pallas_call x2, Pallas kernels, attn_backward(): pl.pallas_call(attn_backward_kernel, out_shape=tuple((jax.ShapeDtypeStruc...  79.2 us
    pallas_call x2, Pallas kernels, attn_forward(): pl.pallas_call(attn_forward_kernel, out_shape=tuple((jax.ShapeDtypeStruct...  41.4 us

profile of v2, /device:TPU:0, one launch (start us, length us, event | category | flops | bytes accessed | tf_op | source)
XLA Modules:
  0.0 451.4 jit_solution(1977625588553611604)
XLA Ops:
  3.1 1.3 select_maximum_fusion.gains_ref
  5.4 0.9 pad_maximum_fusion.2.trig_ref
  6.3 2.0 copy.34.w_down_ref
  8.3 1.2 bitcast_convert_fusion.1.res_ref
  10.2 1.2 copy.33
  11.4 1.3 bitcast_convert_fusion.up_ref
  13.4 2.1 pad_maximum_fusion.w_kvq_ref
  15.5 21.6 %attn_forward.2 = (bf16[320,960]{1,0:T(8,128)(2,1)}, bf16[15,320,128]{2,1,0:T(8,128)(2,1)}, bf16[4,320,640]{2,1,0:T(8,128)(2,1)}, f32[5,1,960]{2,1,0:T(1,128)}, ...) custom-call(f32[320,960]{1,0:T(8,128)} %bitcast_convert_fusion.1.res_ref, ...), custom_call_target="tpu_custom_call" | custom-call | tf_op jit(solution)/shard_map/attn_forward/pallas_call | solution.py:182
  37.1 43.9 %ffn_forward.2 = (f32[320,960]{1,0:T(8,128)}, bf16[4,320,960]{2,1,0:T(8,128)(2,1)}, bf16[4,320,640]{2,1,0:T(8,128)(2,1)}, bf16[4,320,640]{2,1,0:T(8,128)(2,1)}) custom-call(f32[320,960]{1,0:T(8,128)} %get-tuple-element.48.after_ref, bf16[320,960]{1,0:T(8,128)(2,1)} %get-tuple-element.49.normed_ref, bf16[960,640]{1,0:T(8,128)(2,1)} %w_gate_ref.7, ...), custom_call_target="tpu_custom_call" | custom-call | tf_op jit(solution)/shard_map/ffn_forward/pallas_call | solution.py:296
  81.0 19.8 %attn_forward.3 = (bf16[320,960]{1,0:T(8,128)(2,1)}, bf16[15,320,128]{2,1,0:T(8,128)(2,1)}, bf16[4,320,640]{2,1,0:T(8,128)(2,1)}, f32[5,1,960]{2,1,0:T(1,128)}, ...) custom-call(f32[320,960]{1,0:T(8,128)} %get-tuple-element.50.res_ref, ...), custom_call_target="tpu_custom_call" | custom-call | tf_op jit(solution)/shard_map/attn_forward/pallas_call | solution.py:182
  100.8 44.2 %ffn_forward.3 = (f32[320,960]{1,0:T(8,128)}, bf16[4,320,960]{2,1,0:T(8,128)(2,1)}, bf16[4,320,640]{2,1,0:T(8,128)(2,1)}, bf16[4,320,640]{2,1,0:T(8,128)(2,1)}) custom-call(f32[320,960]{1,0:T(8,128)} %get-tuple-element.51.after_ref, bf16[320,960]{1,0:T(8,128)(2,1)} %get-tuple-element.52.normed_ref, bf16[960,640]{1,0:T(8,128)(2,1)} %w_gate_ref.7, ...), custom_call_target="tpu_custom_call" | custom-call | tf_op jit(solution)/shard_map/ffn_forward/pallas_call | solution.py:296
  145.0 2.3 convert_bitcast_fusion
  147.2 40.9 %ffn_backward.2 = (f32[320,960]{1,0:T(8,128)}, f32[8,960]{1,0:T(8,128)}, f32[3,960,640]{2,1,0:T(8,128)}) custom-call(f32[320,960]{1,0:T(8,128)} %bitcast_convert_fusion.up_ref, f32[320,960]{1,0:T(8,128)} %get-tuple-element.51.after_ref, f32[8,960]{1,0:T(8,128)} %select_maximum_fusion.gains_ref, bf16[4,320,960]{2,1,0:T(8,128)(2,1)} %get-tuple-element.54.rows_ref, ...), custom_call_target="tpu_custom_call" | custom-call | tf_op jit(solution)/shard_map/ffn_backward/pallas_call | solution.py:422
  189.0 37.5 %attn_backward.2 = (f32[320,960]{1,0:T(8,128)}, f32[8,960]{1,0:T(8,128)}, f32[4,960,640]{2,1,0:T(8,128)}) custom-call(f32[320,960]{1,0:T(8,128)} %get-tuple-element.57.after_grad_ref, f32[320,960]{1,0:T(8,128)} %get-tuple-element.50.res_ref, bf16[320,960]{1,0:T(8,128)(2,1)} %get-tuple-element.58.normed_ref, f32[8,960]{1,0:T(8,128)} %select_maximum_fusion.gains_ref, ...), custom_call_target="tpu_custom_call" | custom-call | tf_op jit(solution)/shard_map/attn_backward/pallas_call | solution.py:585
  226.5 49.5 %ffn_backward.3 = (f32[320,960]{1,0:T(8,128)}, f32[8,960]{1,0:T(8,128)}, f32[3,960,640]{2,1,0:T(8,128)}) custom-call(f32[320,960]{1,0:T(8,128)} %get-tuple-element.63.up_ref, f32[320,960]{1,0:T(8,128)} %get-tuple-element.48.after_ref, f32[8,960]{1,0:T(8,128)} %select_maximum_fusion.gains_ref, bf16[4,320,960]{2,1,0:T(8,128)(2,1)} %get-tuple-element.64.rows_ref, ...), custom_call_target="tpu_custom_call" | custom-call | tf_op jit(solution)/shard_map/ffn_backward/pallas_call | solution.py:422
  276.0 41.7 %attn_backward.3 = (f32[320,960]{1,0:T(8,128)}, f32[8,960]{1,0:T(8,128)}, f32[4,960,640]{2,1,0:T(8,128)}) custom-call(f32[320,960]{1,0:T(8,128)} %get-tuple-element.68.after_grad_ref, f32[320,960]{1,0:T(8,128)} %bitcast_convert_fusion.1.res_ref, bf16[320,960]{1,0:T(8,128)(2,1)} %get-tuple-element.69.normed_ref, f32[8,960]{1,0:T(8,128)} %select_maximum_fusion.gains_ref, ...), custom_call_target="tpu_custom_call" | custom-call | tf_op jit(solution)/shard_map/attn_backward/pallas_call | solution.py:585
  317.7 0.8 slice_reduce_fusion.1
  318.6 0.8 slice_reduce_fusion
  321.0 122.9 %reduce_grads.1 = (f32[4,120,640]{2,1,0:T(8,128)}, f32[3,120,640]{2,1,0:T(8,128)}, f32[8,8,128]{2,1,0:T(8,128)}) custom-call(f32[4,8,120,640]{3,2,1,0:T(8,128)} %bitcast.53, f32[3,8,120,640]{3,2,1,0:T(8,128)} %bitcast.54, f32[8,8,128]{2,1,0:T(8,128)} %pad.14.gain_ref), custom_call_target="tpu_custom_call" | custom-call | tf_op jit(solution)/shard_map/reduce_grads/pallas_call | solution.py:700
  443.9 0.8 dynamic-slice_bitcast_fusion
  445.2 2.1 slice_bitcast_fusion
  448.4 0.8 pad_maximum_fusion.4
  449.2 0.8 pad_maximum_fusion.3
  450.1 1.1 copy.40
  (46 shorter events, 9.0 us)
Async XLA Ops:
  5.0 1.3 copy-start.2
  6.3 2.0 copy-start.6
  8.3 1.2 copy-start.4
  8.3 1.8 copy-start.5
  10.2 1.2 copy-start.7
  11.4 2.0 copy-start
  443.9 3.4 copy-start.3
  448.3 1.8 copy-start.1

commit v3 on v2

--- a/solution.py
+++ b/solution.py
@@ -15,6 +15,8 @@
 EPSILON = 1e-05
 THETA = 10000.0
 CHUNKS = 2
+SHARES = 8
+ROWS_PAD = 32
 MASKED = -1e30
 LOW = jnp.bfloat16
 FULL = jnp.float32
@@ -325,13 +327,13 @@
 def ffn_backward_kernel(
     up_ref, after_ref, gains_ref, rows_ref, gate_ref, upp_ref, w_gate_ref, w_up_ref, w_down_ref, *rest
 ):
-    (prev_ref,) = rest[:-14] if len(rest) == 15 else (None,)
+    (prev_ref,) = rest[:-15] if len(rest) == 16 else (None,)
     (
         grad_out, gain_out, weight_out,
-        low_all, gate_grad, up_grad, hidden,
+        weight_sum, low_all, gate_grad, up_grad, hidden,
         mate_send, mate_recv, x_send, x_recv, own_far,
         send_sem, recv_sem,
-    ) = rest[-14:]
+    ) = rest[-15:]
     seq, dp = lax.axis_index("seq"), lax.axis_index("dp")
     core, chip_x = lax.rem(seq, 2), lax.div(seq, 2)
     mate_seq, far_seq = seq + 1 - 2 * core, lax.rem(seq + 2, 4)
@@ -373,10 +375,11 @@
         ):
             term = dot(left, right, TN)
             if not first:
-                term = term + weight_out[i]
+                weight_out[i] = (term + weight_sum[i]).astype(LOW)
             elif prev_ref is not None:
-                term = term + prev_ref[i]
-            weight_out[i] = term
+                weight_sum[i] = term + prev_ref[i].astype(FULL)
+            else:
+                weight_sum[i] = term
 
     everything = pl.ds(0, length)
     grad_out[...] = ffn(seq, everything)
@@ -413,7 +416,7 @@
     shapes = (
         ((length, width), FULL),
         ((8, width), FULL),
-        ((3, width, hidden), FULL),
+        ((3, width, hidden), LOW),
     )
     sems = 3 * CHUNKS + CHUNKS + 2
     args = (upstream, after, gains, rows_all, gate_all, up_all, w_gate, w_up, w_down)
@@ -425,6 +428,7 @@
         in_specs=[VMEM] * len(args),
         out_specs=(VMEM,) * len(shapes),
         scratch_shapes=[
+            pltpu.VMEM((3, width, hidden), FULL),
             pltpu.VMEM((4, length, width), LOW),
             pltpu.VMEM((4, length, hidden), LOW),
             pltpu.VMEM((4, length, hidden), LOW),
@@ -444,17 +448,30 @@
     )(*args)
 
 
+class Hops:
+    def __init__(self, send_sem, recv_sem):
+        self.send_sem, self.recv_sem, self.used = send_sem, recv_sem, 0
+
+    def __call__(self, src, dst, target):
+        index, self.used = self.used, self.used + 1
+        return send(src, dst, self.send_sem.at[index], self.recv_sem.at[index], target)
+
+
 def attn_backward_kernel(
-    after_grad_ref, res_ref, normed_ref, gains_ref, q_ref, kv_ref, log_ref, mixed_ref,
+    last, after_grad_ref, res_ref, normed_ref, gains_ref, q_ref, kv_ref, log_ref, mixed_ref,
     w_kvq_ref, w_out_ref, trig_ref, place_ref, *rest
 ):
-    (prev_ref,) = rest[:-12] if len(rest) == 13 else (None,)
-    (
-        grad_out, gain_out, weight_out,
-        mixed_grad, delta, kv_grad, query_grad, back,
-        grad_send, grad_recv,
-        send_sem, recv_sem,
-    ) = rest[-12:]
+    if last:
+        prev, ffn_ref, gain_ref = rest[:3], rest[3], rest[4]
+        grad_out, gain_out, ffn_out, share_outs = rest[5], rest[6], rest[7], rest[8:11]
+        rest = rest[11:]
+    else:
+        prev = (None, None, None)
+        grad_out, gain_out = rest[:2]
+        parts = rest[2:5]
+        rest = rest[5:]
+    mixed_grad, delta, kv_grad, query_grad, back, grad_send, grad_recv, send_sem, recv_sem = rest[:9]
+    hop = Hops(send_sem, recv_sem)
     seq, dp = lax.axis_index("seq"), lax.axis_index("dp")
     core, chip_x = lax.rem(seq, 2), lax.div(seq, 2)
     mate_seq, far_seq = seq + 1 - 2 * core, lax.rem(seq + 2, 4)
@@ -463,10 +480,96 @@
     length, width = res_ref.shape
     stacked = GROUP * length
     kv_width = 2 * KV_HEADS * HEAD_DIM
-    greet([mate, x_mate])
-
-    def hop(index, src, dst, target):
-        return send(src, dst, send_sem.at[index], recv_sem.at[index], target)
+    if last:
+        parts = rest[9:12]
+        f_y_recv, f_z_send, f_z_recv, gain_recv = rest[12:16]
+        buffers = [rest[16 + 8 * i : 24 + 8 * i] for i in range(3)]
+        row_y, row_z = lax.rem(dp, 2), lax.div(dp, 2)
+        y_mate = device(seq, dp + 1 - 2 * row_y)
+        z_of = [lax.rem(row_z + k, 4) for k in range(1, 4)]
+        z_mates = [device(seq, z * 2 + row_y) for z in z_of]
+        greet([mate, x_mate, y_mate] + z_mates)
+        f_y = [hop(ffn_ref.at[m, :, 1 - row_y], f_y_recv.at[m], y_mate) for m in range(3)]
+    else:
+        greet([mate, x_mate])
+
+    def f_z_start(m):
+        f_y[m].wait()
+        copies = []
+        for k in range(3):
+            joint = ffn_ref[m, z_of[k], row_y].astype(FULL) + f_y_recv[m, z_of[k]].astype(FULL)
+            f_z_send[m, k] = joint.astype(LOW)
+            copies.append(hop(f_z_send.at[m, k], f_z_recv.at[m, k], z_mates[k]))
+        return copies
+
+    def f_z_finish(m, copies):
+        total = ffn_ref[m, row_z, row_y].astype(FULL) + f_y_recv[m, row_z].astype(FULL)
+        for k in range(3):
+            copies[k].wait()
+            total = total + f_z_recv[m, k].astype(FULL)
+        ffn_out[m] = total
+
+    quarter = lambda x, c: pl.ds(pl.multiple_of(64 * x + ROWS_PAD * c, ROWS_PAD), ROWS_PAD)
+
+    def core_start(i):
+        core_recv = buffers[i][0]
+        return [hop(parts[i].at[:, quarter(x, 1 - core)], core_recv.at[x], mate) for x in range(2)]
+
+    def x_start(i, copies):
+        core_recv, x_send, x_recv = buffers[i][:3]
+        for copy in copies:
+            copy.wait()
+        joint = parts[i][:, quarter(1 - chip_x, core)].astype(FULL) + core_recv[1 - chip_x].astype(FULL)
+        x_send[...] = joint.astype(LOW)
+        return hop(x_send, x_recv, x_mate)
+
+    def y_start(i, copy):
+        core_recv, x_send, x_recv, own, y_recv = buffers[i][:5]
+        joint = parts[i][:, quarter(chip_x, core)].astype(FULL) + core_recv[chip_x].astype(FULL)
+        copy.wait()
+        own[...] = (joint + x_recv[...].astype(FULL)).astype(LOW).reshape(own.shape)
+        return hop(own.at[:, 1 - row_y], y_recv, y_mate)
+
+    def z_start(i, copy):
+        own, y_recv, z_send, z_recv = buffers[i][3:7]
+        copy.wait()
+        copies = []
+        for k in range(3):
+            z_send[k] = (own[z_of[k], row_y].astype(FULL) + y_recv[z_of[k]].astype(FULL)).astype(LOW)
+            copies.append(hop(z_send.at[k], z_recv.at[k], z_mates[k]))
+        return copies
+
+    def share_start(i, copies):
+        own, y_recv, z_send, z_recv, gathered = buffers[i][3:8]
+        total = own[row_z, row_y].astype(FULL) + y_recv[row_z].astype(FULL)
+        for k in range(3):
+            copies[k].wait()
+            total = total + z_recv[k].astype(FULL)
+        gathered[seq] = total.astype(LOW)
+        mine = gathered.at[seq]
+        return hop(mine, mine, x_mate), hop(mine, mine, mate)
+
+    def share_pass(i, copies):
+        gathered = buffers[i][7]
+        copies[0].wait()
+        theirs = gathered.at[far_seq]
+        return hop(theirs, theirs, mate), copies[1]
+
+    def share_finish(i, copies):
+        gathered = buffers[i][7]
+        for copy in copies:
+            copy.wait()
+        for s in range(4):
+            share_outs[i][s * ROWS_PAD : (s + 1) * ROWS_PAD] = gathered[s].astype(FULL)
+
+    def weight(i, left, right):
+        term = dot(left, right, TN)
+        share = width // SHARES
+        for j in range(SHARES):
+            rows = term[j * share : (j + 1) * share]
+            if prev[i] is not None:
+                rows = rows + prev[i][j, :share].astype(FULL)
+            parts[i][j, :share] = rows.astype(LOW)
 
     low_grad = after_grad_ref[...].astype(LOW)
     mixed_back = dot(low_grad, w_out_ref[...], NT)
@@ -489,6 +592,9 @@
     for g in range(KV_HEADS):
         delta[g] = jnp.concatenate([sums[3 * g + i : 3 * g + i + 1] for i in range(GROUP)], axis=1)
     query_grad[...] = jnp.zeros_like(query_grad)
+    weight(0, mixed_ref[...], low_grad)
+    if last:
+        o_core = core_start(0)
 
     start, place = place_ref[0:1, :], place_ref[1:2, :]
 
@@ -523,14 +629,19 @@
     right = chip_x == 1
     attend_all(far_mate, right)
     grad_send[0] = kv_grad[far_mate].astype(LOW)
-    joint = hop(0, grad_send.at[0], grad_recv.at[0], mate)
+    joint = hop(grad_send.at[0], grad_recv.at[0], mate)
     attend_all(far_seq, right)
     joint.wait()
     grad_send[1] = (kv_grad[far_seq] + grad_recv[0].astype(FULL)).astype(LOW)
-    across = hop(1, grad_send.at[1], grad_recv.at[1], x_mate)
+    across = hop(grad_send.at[1], grad_recv.at[1], x_mate)
+    if last:
+        o_x = x_start(0, o_core)
+        f_z = [f_z_start(0)]
     attend_all(mate_seq, core == 1)
     grad_send[2] = kv_grad[mate_seq].astype(LOW)
-    beside = hop(2, grad_send.at[2], grad_recv.at[2], mate)
+    beside = hop(grad_send.at[2], grad_recv.at[2], mate)
+    if last:
+        f_z.append(f_z_start(1))
     attend_all(seq, seq >= 0, True)
 
     for g in range(KV_HEADS):
@@ -542,19 +653,14 @@
             turned = part * trig_ref[0] - swap_halves(part) * trig_ref[1]
             at = kv_width + h * HEAD_DIM
             back[:, at : at + HEAD_DIM] = turned[:, :HEAD_DIM].astype(LOW)
-
-    def weight(block, at, left, right):
-        columns = slice(at, at + right.shape[1])
-        term = dot(left, right, TN)
-        weight_out[block, :, columns] = term if prev_ref is None else term + prev_ref[block, :, columns]
-
-    third = width // 3
-    cut = kv_width + 2 * third
-    weight(2, 0, mixed_ref[...], low_grad[:, : 2 * third])
-    weight(3, third, mixed_ref[...], low_grad[:, 2 * third :])
-    weight(1, 0, normed_ref[...], back[:, kv_width:cut])
-    weight(3, 0, normed_ref[...], back[:, cut:])
+    weight(1, normed_ref[...], back[:, kv_width:])
+    if last:
+        q_core = core_start(1)
+        o_y = y_start(0, o_x)
+        f_z.append(f_z_start(2))
     normed_grad = dot(back[:, kv_width:], w_kvq_ref[:, kv_width:], NT)
+    if last:
+        q_x = x_start(1, q_core)
 
     across.wait()
     beside.wait()
@@ -562,182 +668,119 @@
     for g in range(KV_HEADS):
         part = own[:, g * 128 : (g + 1) * 128]
         back[:, g * 128 : (g + 1) * 128] = (part * trig_ref[2] - swap_halves(part) * trig_ref[3]).astype(LOW)
-    weight(0, 0, normed_ref[...], back[:, :kv_width])
+    weight(2, normed_ref[...], back[:, :kv_width])
+    if last:
+        kv_core = core_start(2)
     normed_grad = normed_grad + dot(back[:, :kv_width], w_kvq_ref[:, :kv_width], NT)
     sent_back, gain_term = norm_back(res_ref[...], gains_ref[0:1, :], normed_grad)
     grad_out[...] = after_grad_ref[...] + sent_back
-    gain_out[...] = jnp.broadcast_to(gain_term, gain_out.shape)
-
-
-def attn_backward(
-    after_grad, residual, normed, gains, q, kv, log_total, mixed, w_kvq, w_out, trig, place, prev=None
-):
+    if not last:
+        gain_out[...] = jnp.broadcast_to(gain_term, gain_out.shape)
+        return
+
+    row = lax.broadcasted_iota(jnp.int32, gain_out.shape, 0)
+    gain_out[...] = gain_ref[...] + jnp.where(row == 0, gain_term, 0.0)
+    partners = [
+        mate, x_mate, y_mate, device(seq, lax.rem(dp + 4, 8)), device(seq, dp + 2 - 4 * lax.rem(row_z, 2))
+    ]
+    gain_hop = lambda n: hop(gain_out, gain_recv.at[n], partners[n])
+
+    def gain_add(n, copy):
+        copy.wait()
+        gain_out[...] += gain_recv[n]
+
+    kv_x = x_start(2, kv_core)
+    gain_copy = gain_hop(0)
+    o_z = z_start(0, o_y)
+    gain_add(0, gain_copy)
+    gain_copy = gain_hop(1)
+    q_y = y_start(1, q_x)
+    gain_add(1, gain_copy)
+    gain_copy = gain_hop(2)
+    f_z_finish(0, f_z[0])
+    f_z_finish(1, f_z[1])
+    gain_add(2, gain_copy)
+    gain_copy = gain_hop(3)
+    kv_y = y_start(2, kv_x)
+    q_z = z_start(1, q_y)
+    gain_add(3, gain_copy)
+    gain_copy = gain_hop(4)
+    f_z_finish(2, f_z[2])
+    o_s = share_start(0, o_z)
+    kv_z = z_start(2, kv_y)
+    o_s = share_pass(0, o_s)
+    q_s = share_start(1, q_z)
+    gain_add(4, gain_copy)
+    kv_s = share_start(2, kv_z)
+    q_s = share_pass(1, q_s)
+    share_finish(0, o_s)
+    kv_s = share_pass(2, kv_s)
+    share_finish(1, q_s)
+    share_finish(2, kv_s)
+
+
+def attn_backward(after_grad, residual, normed, gains, q, kv, log_total, mixed, w_kvq, w_out, trig, place, final=None):
     length, width = residual.shape
     kv_width = 2 * KV_HEADS * HEAD_DIM
+    last = final is not None
     args = (after_grad, residual, normed, gains, q, kv, log_total, mixed, w_kvq, w_out, trig, place)
-    if prev is not None:
-        args = args + (prev,)
-    shapes = (
-        ((length, width), FULL),
-        ((8, width), FULL),
-        ((4, width, kv_width), FULL),
-    )
+    shapes = (((length, width), FULL), ((8, width), FULL))
+    sizes = (width, width, kv_width)
+    part_shapes = [((SHARES, 4 * ROWS_PAD, c), LOW) for c in sizes]
+    scratch = [
+        pltpu.VMEM((HEADS, length, 128), LOW),
+        pltpu.VMEM((KV_HEADS, 1, GROUP * length), FULL),
+        pltpu.VMEM((4, length, kv_width), FULL),
+        pltpu.VMEM((KV_HEADS, HEAD_DIM, GROUP * length), FULL),
+        pltpu.VMEM((length, kv_width + width), LOW),
+        pltpu.VMEM((3, length, kv_width), LOW),
+        pltpu.VMEM((3, length, kv_width), LOW),
+    ]
+    hops = 3
+    if last:
+        share, hidden = final[3].shape[3:]
+        args = args + tuple(final)
+        shapes = shapes + (((3, share, hidden), FULL),) + tuple(((4 * ROWS_PAD, c), FULL) for c in sizes)
+        hops = 3 + 3 + 9 + 5 + 3 * (2 + 1 + 1 + 3 + 3)
+        scratch += [pltpu.SemaphoreType.DMA((hops,))] * 2
+        scratch += [pltpu.VMEM(*s) for s in part_shapes]
+        scratch += [
+            pltpu.VMEM((3, 4, share, hidden), LOW),
+            pltpu.VMEM((3, 3, share, hidden), LOW),
+            pltpu.VMEM((3, 3, share, hidden), LOW),
+            pltpu.VMEM((5, 8, width), FULL),
+        ]
+        for c in sizes:
+            scratch += [
+                pltpu.VMEM((2, SHARES, ROWS_PAD, c), LOW),
+                pltpu.VMEM((SHARES, ROWS_PAD, c), LOW),
+                pltpu.VMEM((SHARES, ROWS_PAD, c), LOW),
+                pltpu.VMEM((4, 2, ROWS_PAD, c), LOW),
+                pltpu.VMEM((4, ROWS_PAD, c), LOW),
+                pltpu.VMEM((3, ROWS_PAD, c), LOW),
+                pltpu.VMEM((3, ROWS_PAD, c), LOW),
+                pltpu.VMEM((4, ROWS_PAD, c), LOW),
+            ]
+    else:
+        shapes = shapes + tuple(part_shapes)
+        scratch += [pltpu.SemaphoreType.DMA((hops,))] * 2
     return pl.pallas_call(
-        attn_backward_kernel,
+        functools.partial(attn_backward_kernel, last),
         out_shape=tuple(jax.ShapeDtypeStruct(*s) for s in shapes),
         in_specs=[VMEM] * len(args),
         out_specs=(VMEM,) * len(shapes),
-        scratch_shapes=[
-            pltpu.VMEM((HEADS, length, 128), LOW),
-            pltpu.VMEM((KV_HEADS, 1, GROUP * length), FULL),
-            pltpu.VMEM((4, length, kv_width), FULL),
-            pltpu.VMEM((KV_HEADS, HEAD_DIM, GROUP * length), FULL),
-            pltpu.VMEM((length, kv_width + width), LOW),
-            pltpu.VMEM((3, length, kv_width), LOW),
-            pltpu.VMEM((3, length, kv_width), LOW),
-            pltpu.SemaphoreType.DMA((3,)),
-            pltpu.SemaphoreType.DMA((3,)),
-        ],
+        scratch_shapes=scratch,
         compiler_params=pltpu.CompilerParams(
-            collective_id=5 if prev is None else 6, has_side_effects=True, vmem_limit_bytes=60 * 1024 * 1024
+            collective_id=6 if last else 5, has_side_effects=True, vmem_limit_bytes=60 * 1024 * 1024
         ),
-        name="attn_backward",
+        name="attn_backward_last" if last else "attn_backward",
     )(*args)
 
 
-def reduce_kernel(
-    attn_ref, ffn_ref, gain_ref,
-    attn_out, ffn_out, gain_out,
-    core_send, core_recv, x_send, x_recv, own,
-    y_send, y_recv, z_send, z_recv, g_recv, share_low,
-    send_sem, recv_sem,
-):
-    seq, dp = lax.axis_index("seq"), lax.axis_index("dp")
-    core, chip_x = lax.rem(seq, 2), lax.div(seq, 2)
-    row_y, row_z = lax.rem(dp, 2), lax.div(dp, 2)
-    mate = device(seq + 1 - 2 * core, dp)
-    x_mate = device(lax.rem(seq + 2, 4), dp)
-    y_mate = device(seq, dp + 1 - 2 * row_y)
-    z_of = [lax.rem(row_z + k, 4) for k in range(1, 4)]
-    z_mates = [device(seq, z * 2 + row_y) for z in z_of]
-    greet([mate, x_mate, y_mate] + z_mates)
-    low = jnp.bfloat16
-
-    def y_start(index, load):
-        for z in range(4):
-            y_send[index, z] = load(2 * z + 1 - row_y).astype(low)
-        return send(y_send.at[index], y_recv.at[index], send_sem.at[index], recv_sem.at[index], y_mate)
-
-    def z_start(index, load):
-        copies = []
-        for k in range(3):
-            z = z_of[k]
-            z_send[index, k] = (load(2 * z + row_y) + y_recv[index, z].astype(jnp.float32)).astype(low)
-            sem = 4 + 3 * index + k
-            copies.append(
-                send(z_send.at[index, k], z_recv.at[index, k], send_sem.at[sem], recv_sem.at[sem], z_mates[k])
-            )
-        return copies
-
-    def z_finish(index, load, copies):
-        total = load(2 * row_z + row_y) + y_recv[index, row_z].astype(jnp.float32)
-        for k in range(3):
-            copies[k].wait()
-            total = total + z_recv[index, k].astype(jnp.float32)
-        return total
-
-    gain_out[...] = gain_ref[...]
-    hops = [mate, x_mate, y_mate, device(seq, lax.rem(dp + 4, 8)), device(seq, dp + 2 - 4 * lax.rem(row_z, 2))]
-
-    def gain_start(hop):
-        sem = 22 + hop
-        return send(gain_ref if hop == 0 else gain_out, g_recv.at[hop], send_sem.at[sem], recv_sem.at[sem], hops[hop])
-
-    for half in range(2):
-        core_send[half] = attn_ref[2 * half + 1 - core].astype(low)
-    core_copy = send(core_send, core_recv, send_sem.at[16], recv_sem.at[16], mate)
-    gain_copy = gain_start(0)
-    ffn_load = lambda m: (lambda j: ffn_ref[m, j])
-    y_copies = [y_start(m, ffn_load(m)) for m in range(3)]
-    core_copy.wait()
-    x_send[...] = (
-        attn_ref[2 * (1 - chip_x) + core] + core_recv[1 - chip_x].astype(jnp.float32)
-    ).astype(low)
-    x_copy = send(x_send, x_recv, send_sem.at[17], recv_sem.at[17], x_mate)
-    own[...] = attn_ref[seq] + core_recv[chip_x].astype(jnp.float32)
-    for hop in range(5):
-        gain_copy.wait()
-        gain_out[...] += g_recv[hop]
-        if hop < 4:
-            gain_copy = gain_start(hop + 1)
-    z_copies = []
-    for m in range(3):
-        y_copies[m].wait()
-        z_copies.append(z_start(m, ffn_load(m)))
-    x_copy.wait()
-    own[...] += x_recv[...].astype(jnp.float32)
-    own_load = lambda j: own[j]
-    y_copy = y_start(3, own_load)
-    for m in range(3):
-        ffn_out[m] = z_finish(m, ffn_load(m), z_copies[m])
-    y_copy.wait()
-    z_copy = z_start(3, own_load)
-    share_low[seq] = z_finish(3, own_load, z_copy).astype(low)
-    to_mate = send(share_low.at[seq], share_low.at[seq], send_sem.at[18], recv_sem.at[18], mate)
-    to_x = send(share_low.at[seq], share_low.at[seq], send_sem.at[19], recv_sem.at[19], x_mate)
-    to_x.wait()
-    far = lax.rem(seq + 2, 4)
-    onward = send(share_low.at[far], share_low.at[far], send_sem.at[20], recv_sem.at[20], mate)
-    to_mate.wait()
-    onward.wait()
-    attn_out[...] = share_low[...].astype(jnp.float32)
-
-
-def reduce_grads(attn_grads, ffn_grads, gain_grads):
-    share, cols = attn_grads.shape[2:]
-    low, full = jnp.bfloat16, jnp.float32
-    vmem = pl.BlockSpec(memory_space=pltpu.VMEM)
-    return pl.pallas_call(
-        reduce_kernel,
-        out_shape=(
-            jax.ShapeDtypeStruct((4, share, cols), full),
-            jax.ShapeDtypeStruct((3, share, cols), full),
-            jax.ShapeDtypeStruct(gain_grads.shape, full),
-        ),
-        in_specs=[vmem] * 3,
-        out_specs=(vmem, vmem, vmem),
-        scratch_shapes=[
-            pltpu.VMEM((2, 8, share, cols), low),
-            pltpu.VMEM((2, 8, share, cols), low),
-            pltpu.VMEM((8, share, cols), low),
-            pltpu.VMEM((8, share, cols), low),
-            pltpu.VMEM((8, share, cols), full),
-            pltpu.VMEM((4, 4, share, cols), low),
-            pltpu.VMEM((4, 4, share, cols), low),
-            pltpu.VMEM((4, 3, share, cols), low),
-            pltpu.VMEM((4, 3, share, cols), low),
-            pltpu.VMEM((5,) + gain_grads.shape, full),
-            pltpu.VMEM((4, share, cols), low),
-            pltpu.SemaphoreType.DMA((27,)),
-            pltpu.SemaphoreType.DMA((27,)),
-        ],
-        compiler_params=pltpu.CompilerParams(
-            collective_id=0, has_side_effects=True, vmem_limit_bytes=60 * 1024 * 1024
-        ),
-        name="reduce_grads",
-    )(attn_grads, ffn_grads, gain_grads)
-
-
-def unpack(grads):
-    rows, columns = grads.shape[1:]
-    pairs = grads[0].reshape(rows, KV_HEADS, 2, HEAD_DIM)
-    half = columns // 2
-    return (
-        jnp.concatenate([grads[1], grads[3][:, :half]], axis=1),
-        pairs[:, :, 0].reshape(rows, -1),
-        pairs[:, :, 1].reshape(rows, -1),
-        jnp.concatenate([grads[2], grads[3][:, half:]], axis=1),
-    )
+def split_pairs(grads):
+    rows = grads.shape[0]
+    pairs = grads.reshape(rows, KV_HEADS, 2, HEAD_DIM)
+    return pairs[:, :, 0].reshape(rows, -1), pairs[:, :, 1].reshape(rows, -1)
 
 
 def on_device(
@@ -769,26 +812,27 @@
         residual = result
     output = residual.astype(LOW)
     upstream = cotangent[0].astype(FULL)
-    ffn_grads, attn_grads, gain_terms = None, None, []
+    share = width // SHARES
+    ffn_grads, parts, gain_grads = None, None, None
+    whole = lax.axis_size("dp") != SHARES
     for repeat in (1, 0):
         residual, normed, q, kv, log_total, mixed, after, rows_all, gate_all, up_all = kept[repeat]
         after_grad, ffn_gain_term, ffn_grads = ffn_backward(
             upstream, after, gains, rows_all, gate_all, up_all, w_gate, w_up, w_down, ffn_grads
         )
-        upstream, attn_gain_term, attn_grads = attn_backward(
-            after_grad, residual, normed, gains, q, kv, log_total, mixed, w_kvq, w_out, trig, place, attn_grads
-        )
-        gain_terms.append(jnp.stack([attn_gain_term[0], ffn_gain_term[0]]))
-    gain_grads = gain_terms[0] + gain_terms[1]
-    if lax.axis_size("dp") == 8 and width % 64 == 0:
-        share = width // 8
-        own = gain_grads.reshape(2, 8, share).transpose(1, 0, 2)
-        own = jnp.pad(own, ((0, 0), (0, 6), (0, 128 - share)))
-        attn_share, ffn_share, gain_share = reduce_grads(
-            attn_grads.reshape(4, 8, share, -1), ffn_grads.reshape(3, 8, share, -1), own
-        )
-        own_gains = lax.dynamic_index_in_dim(gain_share, lax.axis_index("dp"), 0, keepdims=False)[:2, :share]
-    else:
+        args = (after_grad, residual, normed, gains, q, kv, log_total, mixed, w_kvq, w_out, trig, place)
+        if repeat == 1:
+            upstream, attn_gain_term, *parts = attn_backward(*args)
+            gain_grads = jnp.stack([attn_gain_term[0], ffn_gain_term[0]])
+        elif whole:
+            upstream, attn_gain_term, *terms = attn_backward(*args)
+            gain_grads = gain_grads + jnp.stack([attn_gain_term[0], ffn_gain_term[0]])
+            parts = [part.astype(FULL) + term.astype(FULL) for part, term in zip(parts, terms)]
+        else:
+            gain_grads = gain_grads + jnp.stack([jnp.zeros_like(attn_gain), ffn_gain_term[0]])
+            final = (*parts, ffn_grads.reshape(3, SHARES // 2, 2, share, -1), jnp.pad(gain_grads, ((0, 6), (0, 0))))
+            upstream, gain_all, ffn_share, *shares = attn_backward(*args, final)
+    if whole:
 
         def over_rows(grads, dim):
             grads = lax.psum_scatter(grads.astype(LOW), "dp", scatter_dimension=dim, tiled=True)
@@ -797,18 +841,21 @@
         def over_all(grads, dim):
             return lax.psum(over_rows(grads, dim).astype(LOW), "seq").astype(FULL)
 
-        attn_share = over_all(attn_grads, 1)
+        shares = [over_all(part[:, :share].reshape(width, -1), 0) for part in parts]
         ffn_share = over_rows(ffn_grads, 1)
         own_gains = over_all(gain_grads, 1)
-    query_share, key_share, value_share, out_share = unpack(attn_share)
+    else:
+        shares = [part[:share] for part in shares]
+        own_gains = lax.dynamic_slice_in_dim(gain_all, lax.axis_index("dp") * share, share, axis=1)
+    key_share, value_share = split_pairs(shares[2])
     return (
         output[None],
         upstream[None],
         own_gains[0],
-        query_share,
+        shares[1],
         key_share,
         value_share,
-        out_share,
+        shares[0],
         own_gains[1],
         ffn_share[0],
         ffn_share[1],

time: 459 us -> 382 us (0.83)
  Pallas kernels: 422 us -> 348 us
    pallas_call x3 -> x2, Pallas kernels: 202 us -> 132 us  [attn_backward(): pl.pallas_call(functools.partial(attn_backward_kernel, last), out_shape=t...]
    pallas_call x2, Pallas kernels: 90.4 us -> 85.8 us  [ffn_backward(): pl.pallas_call(ffn_backward_kernel, out_shape=tuple((jax.ShapeDtypeStruct...]
where the time goes in v3:
time: 382 us; the launch traced here: 376 us
  Pallas kernels  348 us (91%)
  local copies, waits for them, and re-layouts  15.4 us (4%)
  other arithmetic  11.5 us (3%)
    pallas_call x2, Pallas kernels, attn_backward(): pl.pallas_call(functools.partial(attn_backward_kernel, last), out_shape=t...  132 us
    pallas_call x2, Pallas kernels, ffn_forward(): pl.pallas_call(ffn_forward_kernel, out_shape=tuple((jax.ShapeDtypeStruct(...  88.1 us
    pallas_call x2, Pallas kernels, ffn_backward(): pl.pallas_call(ffn_backward_kernel, out_shape=tuple((jax.ShapeDtypeStruct...  85.8 us
    pallas_call x2, Pallas kernels, attn_forward(): pl.pallas_call(attn_forward_kernel, out_shape=tuple((jax.ShapeDtypeStruct...  41.5 us

profile of v3, /device:TPU:0, one launch (start us, length us, event | category | flops | bytes accessed | tf_op | source)
XLA Modules:
  0.0 375.5 jit_solution(14829826455482243825)
XLA Ops:
  3.1 1.3 select_maximum_fusion.gains_ref
  5.4 0.9 pad_maximum_fusion.2.trig_ref
  6.3 1.9 copy.34.w_down_ref
  8.3 1.2 bitcast_convert_fusion.1.res_ref
  10.2 1.2 copy.33
  11.3 1.2 bitcast_convert_fusion.up_ref
  12.6 0.8 copy-done
  13.4 2.1 pad_maximum_fusion.w_kvq_ref
  15.4 21.9 %attn_forward.2 = (bf16[320,960]{1,0:T(8,128)(2,1)}, bf16[15,320,128]{2,1,0:T(8,128)(2,1)}, bf16[4,320,640]{2,1,0:T(8,128)(2,1)}, f32[5,1,960]{2,1,0:T(1,128)}, ...) custom-call(f32[320,960]{1,0:T(8,128)} %bitcast_convert_fusion.1.res_ref, ...), custom_call_target="tpu_custom_call" | custom-call | tf_op jit(solution)/shard_map/attn_forward/pallas_call | solution.py:184
  37.3 44.1 %ffn_forward.2 = (f32[320,960]{1,0:T(8,128)}, bf16[4,320,960]{2,1,0:T(8,128)(2,1)}, bf16[4,320,640]{2,1,0:T(8,128)(2,1)}, bf16[4,320,640]{2,1,0:T(8,128)(2,1)}) custom-call(f32[320,960]{1,0:T(8,128)} %get-tuple-element.50.after_ref, bf16[320,960]{1,0:T(8,128)(2,1)} %get-tuple-element.51.normed_ref, bf16[960,640]{1,0:T(8,128)(2,1)} %w_gate_ref.7, ...), custom_call_target="tpu_custom_call" | custom-call | tf_op jit(solution)/shard_map/ffn_forward/pallas_call | solution.py:298
  81.4 19.6 %attn_forward.3 = (bf16[320,960]{1,0:T(8,128)(2,1)}, bf16[15,320,128]{2,1,0:T(8,128)(2,1)}, bf16[4,320,640]{2,1,0:T(8,128)(2,1)}, f32[5,1,960]{2,1,0:T(1,128)}, ...) custom-call(f32[320,960]{1,0:T(8,128)} %get-tuple-element.52.res_ref, ...), custom_call_target="tpu_custom_call" | custom-call | tf_op jit(solution)/shard_map/attn_forward/pallas_call | solution.py:184
  101.0 44.0 %ffn_forward.3 = (f32[320,960]{1,0:T(8,128)}, bf16[4,320,960]{2,1,0:T(8,128)(2,1)}, bf16[4,320,640]{2,1,0:T(8,128)(2,1)}, bf16[4,320,640]{2,1,0:T(8,128)(2,1)}) custom-call(f32[320,960]{1,0:T(8,128)} %get-tuple-element.53.after_ref, bf16[320,960]{1,0:T(8,128)(2,1)} %get-tuple-element.54.normed_ref, bf16[960,640]{1,0:T(8,128)(2,1)} %w_gate_ref.7, ...), custom_call_target="tpu_custom_call" | custom-call | tf_op jit(solution)/shard_map/ffn_forward/pallas_call | solution.py:298
  145.0 2.3 convert_bitcast_fusion
  147.3 40.0 %ffn_backward.2 = (f32[320,960]{1,0:T(8,128)}, f32[8,960]{1,0:T(8,128)}, bf16[3,960,640]{2,1,0:T(8,128)(2,1)}) custom-call(f32[320,960]{1,0:T(8,128)} %bitcast_convert_fusion.up_ref, f32[320,960]{1,0:T(8,128)} %get-tuple-element.53.after_ref, f32[8,960]{1,0:T(8,128)} %select_maximum_fusion.gains_ref, bf16[4,320,960]{2,1,0:T(8,128)(2,1)} %get-tuple-element.56.rows_ref, ...), custom_call_target="tpu_custom_call" | custom-call | tf_op jit(solution)/shard_map/ffn_backward/pallas_call | solution.py:425
  187.3 0.8 slice.40
  188.0 37.2 %attn_backward.1 = (f32[320,960]{1,0:T(8,128)}, f32[8,960]{1,0:T(8,128)}, bf16[8,128,960]{2,1,0:T(8,128)(2,1)}, bf16[8,128,960]{2,1,0:T(8,128)(2,1)}, bf16[8,128,640]{2,1,0:T(8,128)(2,1)}) custom-call(f32[320,960]{1,0:T(8,128)} %get-tuple-element.59.after_grad_ref, f32[320,960]{1,0:T(8,128)} %get-tuple-element.52.res_ref, ...), custom_call_target="tpu_custom_call" | custom-call | tf_op jit(solution)/shard_map/attn_backward/pallas_call | solution.py:767
  225.2 45.8 %ffn_backward.3 = (f32[320,960]{1,0:T(8,128)}, f32[8,960]{1,0:T(8,128)}, bf16[3,960,640]{2,1,0:T(8,128)(2,1)}) custom-call(f32[320,960]{1,0:T(8,128)} %get-tuple-element.65.up_ref, f32[320,960]{1,0:T(8,128)} %get-tuple-element.50.after_ref, f32[8,960]{1,0:T(8,128)} %select_maximum_fusion.gains_ref, bf16[4,320,960]{2,1,0:T(8,128)(2,1)} %get-tuple-element.66.rows_ref, ...), custom_call_target="tpu_custom_call" | custom-call | tf_op jit(solution)/shard_map/ffn_backward/pallas_call | solution.py:425
  273.1 95.2 %attn_backward_last.1 = (f32[320,960]{1,0:T(8,128)}, f32[8,960]{1,0:T(8,128)}, f32[3,120,640]{2,1,0:T(8,128)}, f32[128,960]{1,0:T(8,128)}, f32[128,960]{1,0:T(8,128)}, /*index=5*/f32[128,640]{1,0:T(8,128)}) custom-call(f32[320,960]{1,0:T(8,128)} %get-tuple-element.70.after_grad_ref, f32[320,960]{1,0:T(8,128)} %bitcast_convert_fusion.1.res_ref, ...), custom_call_target="tpu_custom_call" | custom-call | tf_op jit(solution)/shard_map/attn_backward_last/pallas_call | solution.py:767
  368.3 0.8 constant_dynamic-slice_fusion
  369.7 1.0 slice.44
  371.7 0.8 slice.43
  372.5 0.8 slice.47
  373.3 0.9 slice_bitcast_fusion
  374.3 1.1 copy.40
  (43 shorter events, 7.7 us)
Async XLA Ops:
  5.0 1.3 copy-start.2
  6.3 1.9 copy-start.6
  8.3 1.2 copy-start.4
  8.3 1.8 copy-start.5
  10.2 1.2 copy-start.7
  11.3 2.0 copy-start
  368.3 3.3 copy-start.9
  369.7 2.8 copy-start.8
  370.9 2.4 copy-start.3
  372.5 1.8 copy-start.1

commit v4 on v3

--- a/solution.py
+++ b/solution.py
@@ -17,6 +17,7 @@
 CHUNKS = 2
 SHARES = 8
 ROWS_PAD = 32
+PIECE = 128
 MASKED = -1e30
 LOW = jnp.bfloat16
 FULL = jnp.float32
@@ -42,6 +43,15 @@
     return copy
 
 
+class Hops:
+    def __init__(self, send_sem, recv_sem):
+        self.send_sem, self.recv_sem, self.used = send_sem, recv_sem, 0
+
+    def __call__(self, src, dst, target):
+        index, self.used = self.used, self.used + 1
+        return send(src, dst, self.send_sem.at[index], self.recv_sem.at[index], target)
+
+
 def greet(targets):
     barrier = pltpu.get_barrier_semaphore()
     for target in targets:
@@ -55,6 +65,10 @@
     return lax.dot_general(left, right, dims, preferred_element_type=FULL)
 
 
+def cost(microseconds):
+    return pl.CostEstimate(flops=int(microseconds * 1.15e9), bytes_accessed=1 << 20, transcendentals=0)
+
+
 def inverse_rms(value):
     return lax.rsqrt(jnp.mean(value * value, axis=-1, keepdims=True) + EPSILON)
 
@@ -66,10 +80,15 @@
 
 
 def attn_forward_kernel(
-    res_ref, gains_ref, w_kvq_ref, w_out_ref, trig_ref, place_ref,
-    normed_out, q_out, kv_out, log_out, mixed_out, after_out, normed_two_out,
-    peak, total, acc, send_sem, recv_sem,
+    extra, res_ref, gains_ref, w_kvq_ref, w_out_ref, trig_ref, place_ref, *rest
 ):
+    if extra:
+        extra_ref, extra_out = rest[0], rest[8]
+        rest = rest[1:8] + rest[9:]
+    (
+        normed_out, q_out, kv_out, log_out, mixed_out, after_out, normed_two_out,
+        peak, total, acc, send_sem, recv_sem,
+    ) = rest[:12]
     seq, dp = lax.axis_index("seq"), lax.axis_index("dp")
     core, chip_x = lax.rem(seq, 2), lax.div(seq, 2)
     mate_seq, far_seq = seq + 1 - 2 * core, lax.rem(seq + 2, 4)
@@ -140,6 +159,12 @@
     to_x.wait()
     far_kv = kv_out.at[far_seq]
     onward = send(far_kv, far_kv, send_sem.at[2], recv_sem.at[2], mate)
+    if extra:
+        mine, theirs = extra_out.at[seq], extra_out.at[far_seq]
+        keep = pltpu.make_async_copy(extra_ref, mine, rest[12])
+        keep.start()
+        extra_x = send(extra_ref, mine, send_sem.at[3], recv_sem.at[3], x_mate)
+        extra_mate = send(extra_ref, mine, send_sem.at[4], recv_sem.at[4], mate)
 
     @pl.when(chip_x == 1)
     def _():
@@ -164,12 +189,19 @@
     after = residual + dot(mixed_out[...], w_out_ref[...])
     after_out[...] = after
     normed_two_out[...] = (after * inverse_rms(after) * gains_ref[1:2, :]).astype(LOW)
+    if extra:
+        extra_x.wait()
+        extra_onward = send(theirs, theirs, send_sem.at[5], recv_sem.at[5], mate)
+        keep.wait()
+        extra_mate.wait()
+        extra_onward.wait()
 
 
 VMEM = pl.BlockSpec(memory_space=pltpu.VMEM)
-
-
-def attn_forward(residual, gains, w_kvq, w_out, trig, place):
+ANYWHERE = pl.BlockSpec(memory_space=pl.ANY)
+
+
+def attn_forward(residual, gains, w_kvq, w_out, trig, place, extra=None):
     length, width = residual.shape
     kv_width = 2 * KV_HEADS * HEAD_DIM
     shapes = (
@@ -181,23 +213,31 @@
         ((length, width), FULL),
         ((length, width), LOW),
     )
+    args = (residual, gains, w_kvq, w_out, trig, place)
+    in_specs, out_specs, extra_scratch, hops = [VMEM] * 6, (VMEM,) * 7, [], 3
+    if extra is not None:
+        args, in_specs, out_specs = args + (extra,), in_specs + [ANYWHERE], out_specs + (ANYWHERE,)
+        shapes = shapes + (((4,) + extra.shape, extra.dtype),)
+        extra_scratch, hops = [pltpu.SemaphoreType.DMA], 6
     return pl.pallas_call(
-        attn_forward_kernel,
+        functools.partial(attn_forward_kernel, extra is not None),
         out_shape=tuple(jax.ShapeDtypeStruct(*s) for s in shapes),
-        in_specs=[VMEM] * 6,
-        out_specs=(VMEM,) * len(shapes),
+        in_specs=in_specs,
+        out_specs=out_specs,
         scratch_shapes=[
             pltpu.VMEM((KV_HEADS, 1, GROUP * length), FULL),
             pltpu.VMEM((KV_HEADS, 1, GROUP * length), FULL),
             pltpu.VMEM((KV_HEADS, HEAD_DIM, GROUP * length), FULL),
-            pltpu.SemaphoreType.DMA((3,)),
-            pltpu.SemaphoreType.DMA((3,)),
-        ],
+            pltpu.SemaphoreType.DMA((hops,)),
+            pltpu.SemaphoreType.DMA((hops,)),
+        ]
+        + extra_scratch,
         compiler_params=pltpu.CompilerParams(
-            collective_id=1, has_side_effects=True, vmem_limit_bytes=60 * 1024 * 1024
+            collective_id=1 if extra is None else 0, has_side_effects=True, vmem_limit_bytes=60 * 1024 * 1024
         ),
+        cost_estimate=cost(25),
         name="attn_forward",
-    )(residual, gains, w_kvq, w_out, trig, place)
+    )(*args)
 
 
 def prepare(positions, w_query, w_key, w_value):
@@ -225,7 +265,7 @@
 
 def ffn_forward_kernel(
     after_ref, normed_ref, w_gate_ref, w_up_ref, w_down_ref,
-    res_out, rows_out, gate_out, up_out,
+    res_out, rows_out,
     mate_send, mate_recv, x_send, x_recv, own_far,
     send_sem, recv_sem,
 ):
@@ -253,10 +293,8 @@
         block = rows_out[quarter, rows]
         gate = dot(block, w_gate_ref[...])
         up = dot(block, w_up_ref[...])
-        gate_out[quarter, rows] = gate.astype(LOW)
-        up_out[quarter, rows] = up.astype(LOW)
         hidden = (gate * jax.nn.sigmoid(gate) * up).astype(LOW)
-        return dot(hidden, w_down_ref[...])
+        return dot(hidden, w_down_ref[...], NT)
 
     everything = pl.ds(0, length)
     res_out[...] = after_ref[...] + ffn(seq, everything)
@@ -287,12 +325,9 @@
 
 def ffn_forward(after, normed_two, w_gate, w_up, w_down):
     length, width = after.shape
-    hidden = w_gate.shape[1]
     shapes = (
         ((length, width), FULL),
         ((4, length, width), LOW),
-        ((4, length, hidden), LOW),
-        ((4, length, hidden), LOW),
     )
     sems = 3 * CHUNKS + CHUNKS + 2
     return pl.pallas_call(
@@ -312,6 +347,7 @@
         compiler_params=pltpu.CompilerParams(
             collective_id=2, has_side_effects=True, vmem_limit_bytes=60 * 1024 * 1024
         ),
+        cost_estimate=cost(36),
         name="ffn_forward",
     )(after, normed_two, w_gate, w_up, w_down)
 
@@ -324,137 +360,164 @@
     return back, jnp.sum(grad * value * inverse, axis=0, keepdims=True)
 
 
-def ffn_backward_kernel(
-    up_ref, after_ref, gains_ref, rows_ref, gate_ref, upp_ref, w_gate_ref, w_up_ref, w_down_ref, *rest
-):
-    (prev_ref,) = rest[:-15] if len(rest) == 16 else (None,)
+def ffn_all_kernel(second, up_ref, after_ref, gains_ref, own_ref, still_refs, gate_ref, upw_ref, down_ref, far_ref, *rest):
+    if second:
+        result_out, prev_ref = rest[0], None
+        rest = rest[1:]
+    else:
+        prev_ref, rest = rest[0], rest[1:]
     (
         grad_out, gain_out, weight_out,
-        weight_sum, low_all, gate_grad, up_grad, hidden,
-        mate_send, mate_recv, x_send, x_recv, own_far,
-        send_sem, recv_sem,
-    ) = rest[-15:]
+        w_in, w_down, still_ref, moved, in_grad, in_temp, hidden, back,
+        load_sem, send_sem, recv_sem,
+    ) = rest
+    hop = Hops(send_sem, recv_sem)
     seq, dp = lax.axis_index("seq"), lax.axis_index("dp")
-    core, chip_x = lax.rem(seq, 2), lax.div(seq, 2)
+    core = lax.rem(seq, 2)
     mate_seq, far_seq = seq + 1 - 2 * core, lax.rem(seq + 2, 4)
     far_mate = lax.rem(mate_seq + 2, 4)
     mate, x_mate = device(mate_seq, dp), device(far_seq, dp)
     length, width = up_ref.shape
-    step = length // CHUNKS
+    units = gate_ref.shape[1]
+    whole = pl.ds(0, width)
+
+    def slots(w, rows):
+        return w_in.at[w, rows, :units], w_in.at[w, rows, units:], w_down.at[w, rows]
+
+    loads = []
+
+    def load(src, dst):
+        loads.append(pltpu.make_async_copy(src, dst, load_sem.at[len(loads)]))
+        loads[-1].start()
+
+    for src, dst in zip((gate_ref, upw_ref, down_ref), slots(0, whole)):
+        load(src, dst)
+    moved[seq] = own_ref[...].astype(LOW)
+    at = 0
+    for ref in still_refs:
+        load(ref, still_ref.at[:, pl.ds(at, ref.shape[1])])
+        at += ref.shape[1]
+    far_from = len(loads)
+    for d in range(SHARES):
+        at = min(d * PIECE, width - PIECE)
+        rows = min(PIECE, width - PIECE - at) if d == SHARES - 2 else PIECE
+        for i, dst in enumerate(slots(2, pl.ds(at, rows))):
+            load(far_ref.at[d, pl.ds(i * PIECE, rows)], dst)
     greet([mate, x_mate])
-    part = lambda k: pl.ds(k * step, step)
-
-    def hop(index, src, dst, target):
-        return send(src, dst, send_sem.at[index], recv_sem.at[index], target)
-
-    low_all[seq] = up_ref[...].astype(LOW)
-    own_rows = lambda k: low_all.at[seq, part(k)]
-    far_rows = lambda k: low_all.at[far_seq, part(k)]
-    to_x = [hop(k, own_rows(k), own_rows(k), x_mate) for k in range(CHUNKS)]
-    to_mate = hop(CHUNKS, low_all.at[seq], low_all.at[seq], mate)
-    base = CHUNKS + 1
-
-    def ffn(quarter, rows):
-        hidden_grad = dot(low_all[quarter, rows], w_down_ref[...], NT)
-        gate = gate_ref[quarter, rows].astype(FULL)
-        up = upp_ref[quarter, rows].astype(FULL)
+    mine, theirs = moved.at[seq], moved.at[far_seq]
+    to_x = hop(mine, mine, x_mate)
+    to_mate = hop(mine, mine, mate)
+    beside = [hop(src, dst, mate) for src, dst in zip((gate_ref, upw_ref, down_ref), slots(1, whole))]
+    rows_ref, low_ref = (moved, still_ref) if second else (still_ref, moved)
+
+    def halves(quarter, w, grads):
+        both = dot(rows_ref[quarter], w_in[w])
+        gate, up = both[:, :units], both[:, units:]
         bend = jax.nn.sigmoid(gate)
         silu = gate * bend
-        hidden[quarter, rows] = (silu * up).astype(LOW)
-        gate_low = (hidden_grad * up * bend * (1.0 + gate * (1.0 - bend))).astype(LOW)
-        up_low = (hidden_grad * silu).astype(LOW)
-        gate_grad[quarter, rows] = gate_low
-        up_grad[quarter, rows] = up_low
-        return dot(gate_low, w_gate_ref[...], NT) + dot(up_low, w_up_ref[...], NT)
-
-    def weights(first_quarter, first):
-        pair = lambda ref: ref[pl.ds(first_quarter, 2)].reshape(2 * length, ref.shape[2])
-        rows, low = pair(rows_ref), pair(low_all)
-        for i, (left, right) in enumerate(
-            ((rows, pair(gate_grad)), (rows, pair(up_grad)), (low, pair(hidden)))
-        ):
-            term = dot(left, right, TN)
-            if not first:
-                weight_out[i] = (term + weight_sum[i]).astype(LOW)
-            elif prev_ref is not None:
-                weight_sum[i] = term + prev_ref[i].astype(FULL)
-            else:
-                weight_sum[i] = term
-
-    everything = pl.ds(0, length)
-    grad_out[...] = ffn(seq, everything)
+        hidden_grad = dot(low_ref[quarter], w_down[w])
+        grads[:, :units] = (hidden_grad * up * bend * (1.0 + gate * (1.0 - bend))).astype(LOW)
+        grads[:, units:] = (hidden_grad * silu).astype(LOW)
+        return (silu * up).astype(LOW)
+
+    for copy in loads[:far_from]:
+        copy.wait()
+    hidden[seq] = halves(seq, 0, in_grad.at[seq])
+    back[...] = dot(in_grad[seq], w_in[0], NT)
+    if second:
+        grad_out[...] = after_ref[...] + dot(hidden[seq], w_down[0], NT)
+    for copy in loads[far_from:]:
+        copy.wait()
+    across = [hop(w_in.at[2], w_in.at[3], mate), hop(w_down.at[2], w_down.at[3], mate)]
+    for copy in beside:
+        copy.wait()
+
+    @pl.loop(1, 4)
+    def _(w):
+        @pl.when(w == 3)
+        def _():
+            for copy in across:
+                copy.wait()
+
+        act = halves(seq, w, in_temp)
+        back[...] += dot(in_temp[...], w_in[w], NT)
+        if second:
+            grad_out[...] += dot(act, w_down[w], NT)
+
+    if second:
+        result_out[...] = grad_out[...].astype(LOW)
+    sent_back, gain_term = norm_back(after_ref[...], gains_ref[1:2, :], back[...])
+    grad_out[...] = up_ref[...].astype(FULL) + sent_back
+    gain_out[...] = jnp.broadcast_to(gain_term, gain_out.shape)
+
     to_mate.wait()
-    mate_send[0] = ffn(mate_seq, everything).astype(LOW)
-    back = hop(base, mate_send.at[0], mate_recv.at[0], mate)
-    last = []
-    for k in range(CHUNKS):
-        to_x[k].wait()
-        onward = hop(base + 1 + k, far_rows(k), far_rows(k), mate)
-        own_far[part(k)] = ffn(far_seq, part(k))
-        onward.wait()
-        mate_send[1, part(k)] = ffn(far_mate, part(k)).astype(LOW)
-        joint = hop(base + 1 + CHUNKS + k, mate_send.at[1, part(k)], mate_recv.at[1, part(k)], mate)
-        joint.wait()
-        x_send[part(k)] = (own_far[part(k)] + mate_recv[1, part(k)].astype(FULL)).astype(LOW)
-        last.append(hop(base + 1 + 2 * CHUNKS + k, x_send.at[part(k)], x_recv.at[part(k)], x_mate))
-        if k == 0:
-            weights(2 * chip_x, True)
-    weights(2 - 2 * chip_x, False)
-    back.wait()
-    total = grad_out[...] + mate_recv[0].astype(FULL)
-    for k in range(CHUNKS):
-        last[k].wait()
-    total = total + x_recv[...].astype(FULL)
-    sent_back, gain_term = norm_back(after_ref[...], gains_ref[1:2, :], total)
-    grad_out[...] = up_ref[...] + sent_back
-    gain_out[...] = jnp.broadcast_to(gain_term, gain_out.shape)
-
-
-def ffn_backward(upstream, after, gains, rows_all, gate_all, up_all, w_gate, w_up, w_down, prev=None):
+    to_x.wait()
+    onward = hop(theirs, theirs, mate)
+
+    @pl.loop(0, 3)
+    def _(i):
+        @pl.when(i == 2)
+        def _():
+            onward.wait()
+
+        quarter = jnp.where(i == 0, mate_seq, jnp.where(i == 1, far_seq, far_mate))
+        hidden[quarter] = halves(quarter, 0, in_grad.at[quarter])
+
+    flat = lambda ref: ref[...].reshape(4 * length, ref.shape[2])
+
+    def finish(i, term):
+        if prev_ref is not None:
+            term = term + prev_ref[i].astype(FULL)
+        weight_out[i] = term.astype(LOW)
+
+    both = dot(flat(rows_ref), flat(in_grad), TN)
+    finish(0, both[:, :units])
+    finish(1, both[:, units:])
+    finish(2, dot(flat(low_ref), flat(hidden), TN))
+
+
+def ffn_all_call(stills, second, *refs):
+    return ffn_all_kernel(second, *refs[:4], refs[4 : 4 + stills], *refs[4 + stills :])
+
+
+def ffn_all(second, upstream, after, gains, own, stills, weights, far, prev=None):
     length, width = after.shape
-    hidden = w_gate.shape[1]
+    units = weights[0].shape[1]
     shapes = (
         ((length, width), FULL),
         ((8, width), FULL),
-        ((3, width, hidden), LOW),
-    )
-    sems = 3 * CHUNKS + CHUNKS + 2
-    args = (upstream, after, gains, rows_all, gate_all, up_all, w_gate, w_up, w_down)
-    if prev is not None:
-        args = args + (prev,)
+        ((3, width, units), LOW),
+    )
+    if second:
+        shapes = (((length, width), LOW),) + shapes
+    args = (upstream, after, gains, own) + tuple(stills) + tuple(weights) + (far,)
+    specs = [VMEM] * 4 + [ANYWHERE] * (len(stills) + 4)
+    if not second:
+        args, specs = args + (prev,), specs + [VMEM]
     return pl.pallas_call(
-        ffn_backward_kernel,
+        functools.partial(ffn_all_call, len(stills), second),
         out_shape=tuple(jax.ShapeDtypeStruct(*s) for s in shapes),
-        in_specs=[VMEM] * len(args),
+        in_specs=specs,
         out_specs=(VMEM,) * len(shapes),
         scratch_shapes=[
-            pltpu.VMEM((3, width, hidden), FULL),
+            pltpu.VMEM((4, width, 2 * units), LOW),
+            pltpu.VMEM((4, width, units), LOW),
             pltpu.VMEM((4, length, width), LOW),
-            pltpu.VMEM((4, length, hidden), LOW),
-            pltpu.VMEM((4, length, hidden), LOW),
-            pltpu.VMEM((4, length, hidden), LOW),
-            pltpu.VMEM((2, length, width), LOW),
-            pltpu.VMEM((2, length, width), LOW),
-            pltpu.VMEM((length, width), LOW),
-            pltpu.VMEM((length, width), LOW),
+            pltpu.VMEM((4, length, width), LOW),
+            pltpu.VMEM((4, length, 2 * units), LOW),
+            pltpu.VMEM((length, 2 * units), LOW),
+            pltpu.VMEM((4, length, units), LOW),
             pltpu.VMEM((length, width), FULL),
-            pltpu.SemaphoreType.DMA((sems,)),
-            pltpu.SemaphoreType.DMA((sems,)),
+            pltpu.SemaphoreType.DMA((3 + len(stills) + 3 * SHARES,)),
+            pltpu.SemaphoreType.DMA((8,)),
+            pltpu.SemaphoreType.DMA((8,)),
         ],
         compiler_params=pltpu.CompilerParams(
-            collective_id=3 if prev is None else 4, has_side_effects=True, vmem_limit_bytes=60 * 1024 * 1024
+            collective_id=3 if second else 4, has_side_effects=True, vmem_limit_bytes=60 * 1024 * 1024
         ),
-        name="ffn_backward",
+        cost_estimate=cost(30),
+        name="ffn_second" if second else "ffn_first_backward",
     )(*args)
-
-
-class Hops:
-    def __init__(self, send_sem, recv_sem):
-        self.send_sem, self.recv_sem, self.used = send_sem, recv_sem, 0
-
-    def __call__(self, src, dst, target):
-        index, self.used = self.used, self.used + 1
-        return send(src, dst, self.send_sem.at[index], self.recv_sem.at[index], target)
 
 
 def attn_backward_kernel(
@@ -640,8 +703,6 @@
     attend_all(mate_seq, core == 1)
     grad_send[2] = kv_grad[mate_seq].astype(LOW)
     beside = hop(grad_send.at[2], grad_recv.at[2], mate)
-    if last:
-        f_z.append(f_z_start(1))
     attend_all(seq, seq >= 0, True)
 
     for g in range(KV_HEADS):
@@ -657,7 +718,6 @@
     if last:
         q_core = core_start(1)
         o_y = y_start(0, o_x)
-        f_z.append(f_z_start(2))
     normed_grad = dot(back[:, kv_width:], w_kvq_ref[:, kv_width:], NT)
     if last:
         q_x = x_start(1, q_core)
@@ -671,6 +731,8 @@
     weight(2, normed_ref[...], back[:, :kv_width])
     if last:
         kv_core = core_start(2)
+        f_z.append(f_z_start(1))
+        kv_x = x_start(2, kv_core)
     normed_grad = normed_grad + dot(back[:, :kv_width], w_kvq_ref[:, :kv_width], NT)
     sent_back, gain_term = norm_back(res_ref[...], gains_ref[0:1, :], normed_grad)
     grad_out[...] = after_grad_ref[...] + sent_back
@@ -689,25 +751,25 @@
         copy.wait()
         gain_out[...] += gain_recv[n]
 
-    kv_x = x_start(2, kv_core)
     gain_copy = gain_hop(0)
-    o_z = z_start(0, o_y)
+    f_z.append(f_z_start(2))
     gain_add(0, gain_copy)
     gain_copy = gain_hop(1)
     q_y = y_start(1, q_x)
+    o_z = z_start(0, o_y)
     gain_add(1, gain_copy)
     gain_copy = gain_hop(2)
+    kv_y = y_start(2, kv_x)
     f_z_finish(0, f_z[0])
-    f_z_finish(1, f_z[1])
     gain_add(2, gain_copy)
     gain_copy = gain_hop(3)
-    kv_y = y_start(2, kv_x)
     q_z = z_start(1, q_y)
+    f_z_finish(1, f_z[1])
     gain_add(3, gain_copy)
     gain_copy = gain_hop(4)
+    kv_z = z_start(2, kv_y)
     f_z_finish(2, f_z[2])
     o_s = share_start(0, o_z)
-    kv_z = z_start(2, kv_y)
     o_s = share_pass(0, o_s)
     q_s = share_start(1, q_z)
     gain_add(4, gain_copy)
@@ -773,6 +835,7 @@
         compiler_params=pltpu.CompilerParams(
             collective_id=6 if last else 5, has_side_effects=True, vmem_limit_bytes=60 * 1024 * 1024
         ),
+        cost_estimate=cost(95 if last else 40),
         name="attn_backward_last" if last else "attn_backward",
     )(*args)
 
@@ -801,37 +864,50 @@
     width = tokens.shape[2]
     trig, w_kvq, place = prepare(positions[0], w_query, w_key, w_value)
     gains = jnp.pad(jnp.stack([attn_gain, ffn_gain]), ((0, 6), (0, 0)))
-    residual = tokens[0].astype(FULL)
-    kept = []
-    for repeat in range(2):
-        normed, q, kv, log_total, mixed, after, normed_two = attn_forward(
-            residual, gains, w_kvq, w_out, trig, place
-        )
-        result, rows_all, gate_all, up_all = ffn_forward(after, normed_two, w_gate, w_up, w_down)
-        kept.append((residual, normed, q, kv, log_total, mixed, after, rows_all, gate_all, up_all))
-        residual = result
-    output = residual.astype(LOW)
-    upstream = cotangent[0].astype(FULL)
+    whole = lax.axis_size("dp") != SHARES
     share = width // SHARES
-    ffn_grads, parts, gain_grads = None, None, None
-    whole = lax.axis_size("dp") != SHARES
-    for repeat in (1, 0):
-        residual, normed, q, kv, log_total, mixed, after, rows_all, gate_all, up_all = kept[repeat]
-        after_grad, ffn_gain_term, ffn_grads = ffn_backward(
-            upstream, after, gains, rows_all, gate_all, up_all, w_gate, w_up, w_down, ffn_grads
-        )
-        args = (after_grad, residual, normed, gains, q, kv, log_total, mixed, w_kvq, w_out, trig, place)
-        if repeat == 1:
-            upstream, attn_gain_term, *parts = attn_backward(*args)
-            gain_grads = jnp.stack([attn_gain_term[0], ffn_gain_term[0]])
-        elif whole:
-            upstream, attn_gain_term, *terms = attn_backward(*args)
-            gain_grads = gain_grads + jnp.stack([attn_gain_term[0], ffn_gain_term[0]])
-            parts = [part.astype(FULL) + term.astype(FULL) for part, term in zip(parts, terms)]
-        else:
-            gain_grads = gain_grads + jnp.stack([jnp.zeros_like(attn_gain), ffn_gain_term[0]])
-            final = (*parts, ffn_grads.reshape(3, SHARES // 2, 2, share, -1), jnp.pad(gain_grads, ((0, 6), (0, 0))))
-            upstream, gain_all, ffn_share, *shares = attn_backward(*args, final)
+    own_weights = (w_gate, w_up, w_down.T)
+
+    def over_x(value):
+        return lax.ppermute(value, "seq", [(s, (s + 2) % 4) for s in range(4)])
+
+    def over_rows_piece(value, d):
+        return lax.dynamic_slice_in_dim(value, jnp.minimum(d * PIECE, width - PIECE), PIECE, axis=0)
+
+    if whole:
+        theirs = [over_x(w) for w in own_weights]
+        far = jnp.stack([jnp.concatenate([over_rows_piece(w, d) for w in theirs]) for d in range(SHARES)])
+    else:
+        piece = jnp.concatenate([over_rows_piece(w, lax.axis_index("dp")) for w in own_weights])
+        far = lax.all_gather(over_x(piece), "dp", axis=0)
+
+    tokens_full = tokens[0].astype(FULL)
+    half = cotangent.shape[1] // 2
+    first = attn_forward(tokens_full, gains, w_kvq, w_out, trig, place, cotangent[0, :half])
+    residual, rows_all = ffn_forward(first[5], first[6], *own_weights)
+    second = attn_forward(residual, gains, w_kvq, w_out, trig, place, cotangent[0, half:])
+    output, after_grad, ffn_gain_term, ffn_grads = ffn_all(
+        True, cotangent[0], second[5], gains, second[6], (first[7], second[7]), own_weights, far
+    )
+
+    def attn_args(after_grad, residual, kept):
+        normed, q, kv, log_total, mixed = kept[:5]
+        return (after_grad, residual, normed, gains, q, kv, log_total, mixed, w_kvq, w_out, trig, place)
+
+    upstream, attn_gain_term, *parts = attn_backward(*attn_args(after_grad, residual, second))
+    gain_grads = jnp.stack([attn_gain_term[0], ffn_gain_term[0]])
+    after_grad, ffn_gain_term, ffn_grads = ffn_all(
+        False, upstream, first[5], gains, upstream, (rows_all,), own_weights, far, ffn_grads
+    )
+    args = attn_args(after_grad, tokens_full, first)
+    if whole:
+        upstream, attn_gain_term, *terms = attn_backward(*args)
+        gain_grads = gain_grads + jnp.stack([attn_gain_term[0], ffn_gain_term[0]])
+        parts = [part.astype(FULL) + term.astype(FULL) for part, term in zip(parts, terms)]
+    else:
+        gain_grads = gain_grads + jnp.stack([jnp.zeros_like(attn_gain), ffn_gain_term[0]])
+        final = (*parts, ffn_grads.reshape(3, SHARES // 2, 2, share, -1), jnp.pad(gain_grads, ((0, 6), (0, 0))))
+        upstream, gain_all, ffn_share, *shares = attn_backward(*args, final)
     if whole:
 
         def over_rows(grads, dim):

time: 382 us -> 357 us (0.935)
  Pallas kernels: 348 us -> 309 us
  between operations: 1.02 us -> 14.4 us
    pallas_call x2 -> x1, Pallas kernels: 88.1 us -> 36 us  [ffn_forward(): pl.pallas_call(ffn_forward_kernel, out_shape=tuple((jax.ShapeDtypeStruct(...]
    pallas_call x4, Pallas kernels: 127 us -> 136 us  [the longest x2 77.3 us: ffn_all(): pl.pallas_call(functools.partial(ffn_all_call, len(stills), second), out_...]
    pallas_call x2, Pallas kernels: 132 us -> 136 us  [attn_backward(): pl.pallas_call(functools.partial(attn_backward_kernel, last), out_shape=t...]
  transfers between devices with their start and end apart: 0 -> 2, of which waited for: 0 -> 1; matrix products, arithmetic and copies ran while one was open for 0% -> 3% of each run, Pallas kernels for 0% -> 27%
where the time goes in v4:
time: 357 us; the launch traced here: 351 us
  Pallas kernels  309 us (87%)
  local copies, waits for them, and re-layouts  15.8 us (4%)
  between operations  14.4 us (4%)
  other arithmetic  8.17 us (2%)
    pallas_call x2, Pallas kernels, attn_backward(): pl.pallas_call(functools.partial(attn_backward_kernel, last), out_shape=t...  136 us
    pallas_call x2, Pallas kernels, ffn_all(): pl.pallas_call(functools.partial(ffn_all_call, len(stills), second), out_...  77.3 us
    pallas_call x2, Pallas kernels, attn_forward(): pl.pallas_call(functools.partial(attn_forward_kernel, extra is not None),...  59 us
    pallas_call x1, Pallas kernels, ffn_forward(): pl.pallas_call(ffn_forward_kernel, out_shape=tuple((jax.ShapeDtypeStruct(...  36 us
  transfers between devices with their start and end apart: 2, of which 1 were waited for; matrix products, arithmetic and copies ran while one was open for 3% of the time, Pallas kernels for 27%

profile of v4, /device:TPU:0, one launch (start us, length us, event | category | flops | bytes accessed | tf_op | source)
XLA Modules:
  0.0 351.2 jit_solution(12445956520696911050)
XLA Ops:
  7.3 1.0 dynamic-slice_bitcast_fusion
  8.3 1.1 constant_dynamic-slice_fusion.1
  9.4 0.8 pad_maximum_fusion.3
  10.2 2.9 collective-permute-start
  13.6 0.9 slice_bitcast_fusion
  14.5 1.2 bitcast_convert_fusion.res_ref
  18.1 1.1 copy.29
  19.2 0.9 pad_maximum_fusion.2.trig_ref
  20.1 3.4 pad_maximum_fusion.w_kvq_ref
  23.6 1.1 collective-permute-done
  24.7 29.7 %attn_forward.2 = (bf16[320,960]{1,0:T(8,128)(2,1)}, bf16[15,320,128]{2,1,0:T(8,128)(2,1)}, bf16[4,320,640]{2,1,0:T(8,128)(2,1)}, f32[5,1,960]{2,1,0:T(1,128)}, ...) custom-call(f32[320,960]{1,0:T(8,128)} %bitcast_convert_fusion.res_ref, ...), custom_call_target="tpu_custom_call" | custom-call | flops 28750000128 | bytes 1048576 | tf_op jit(solution)/shard_map/attn_forward/pallas_call | solution.py:222
  54.4 36.0 %ffn_forward.1 = (f32[320,960]{1,0:T(8,128)}, bf16[4,320,960]{2,1,0:T(8,128)(2,1)}) custom-call(f32[320,960]{1,0:T(8,128)} %get-tuple-element.47.after_ref.refs_1_, bf16[320,960]{1,0:T(8,128)(2,1)} %get-tuple-element.48.normed_ref, bf16[960,640]{1,0:T(8,128)(2,1)} %refs_5_.1, bf16[960,640]{1,0:T(8,128)(2,1)} %refs_6_.3, bf16[960,640]{1,0:T(8,128)(2,1)} %bitcast.56), custom_call_target="tpu_custom_call" | custom-call | flops 41400000512 | bytes 1048576 | tf_op jit(solution)/shard_map/ffn_forward/pallas_call | solution.py:333
  90.5 29.3 %attn_forward.3 = (bf16[320,960]{1,0:T(8,128)(2,1)}, bf16[15,320,128]{2,1,0:T(8,128)(2,1)}, bf16[4,320,640]{2,1,0:T(8,128)(2,1)}, f32[5,1,960]{2,1,0:T(1,128)}, ...) custom-call(f32[320,960]{1,0:T(8,128)} %get-tuple-element.49.res_ref, ...), custom_call_target="tpu_custom_call" | custom-call | flops 28750000128 | bytes 1048576 | tf_op jit(solution)/shard_map/attn_forward/pallas_call | solution.py:222
  119.8 35.3 %ffn_second.1 = (bf16[320,960]{1,0:T(8,128)(2,1)}, f32[320,960]{1,0:T(8,128)}, f32[8,960]{1,0:T(8,128)}, bf16[3,960,640]{2,1,0:T(8,128)(2,1)}) custom-call(bf16[320,960]{1,0:T(8,128)(2,1)} %bitcast.52, f32[320,960]{1,0:T(8,128)} %get-tuple-element.50.refs_1_, f32[8,960]{1,0:T(8,128)} %select_maximum_fusion.gains_ref.refs_2_, ...), custom_call_target="tpu_custom_call" | custom-call | flops 34500001792 | bytes 1048576 | tf_op jit(solution)/shard_map/ffn_second/pallas_call | solution.py:497
  155.9 37.3 %attn_backward.1 = (f32[320,960]{1,0:T(8,128)}, f32[8,960]{1,0:T(8,128)}, bf16[8,128,960]{2,1,0:T(8,128)(2,1)}, bf16[8,128,960]{2,1,0:T(8,128)(2,1)}, bf16[8,128,640]{2,1,0:T(8,128)(2,1)}) custom-call(f32[320,960]{1,0:T(8,128)} %get-tuple-element.55.after_grad_ref, f32[320,960]{1,0:T(8,128)} %get-tuple-element.49.res_ref, ...), custom_call_target="tpu_custom_call" | custom-call | flops 46000001024 | bytes 1048576 | tf_op jit(solution)/shard_map/attn_backward/pallas_call | solution.py:829
  193.2 41.9 %ffn_first_backward.1 = (f32[320,960]{1,0:T(8,128)}, f32[8,960]{1,0:T(8,128)}, bf16[3,960,640]{2,1,0:T(8,128)(2,1)}) custom-call(f32[320,960]{1,0:T(8,128)} %get-tuple-element.61.refs_0_.refs_3_, f32[320,960]{1,0:T(8,128)} %get-tuple-element.47.after_ref.refs_1_, f32[8,960]{1,0:T(8,128)} %select_maximum_fusion.gains_ref.refs_2_, ...), custom_call_target="tpu_custom_call" | custom-call | flops 34500001792 | bytes 1048576 | tf_op jit(solution)/shard_map/ffn_first_backward/pallas_call | solution.py:497
  237.3 99.0 %attn_backward_last.1 = (f32[320,960]{1,0:T(8,128)}, f32[8,960]{1,0:T(8,128)}, f32[3,120,640]{2,1,0:T(8,128)}, f32[128,960]{1,0:T(8,128)}, f32[128,960]{1,0:T(8,128)}, /*index=5*/f32[128,640]{1,0:T(8,128)}) custom-call(f32[320,960]{1,0:T(8,128)} %get-tuple-element.64.after_grad_ref, f32[320,960]{1,0:T(8,128)} %bitcast_convert_fusion.res_ref, ...), custom_call_target="tpu_custom_call" | custom-call | flops 109250002944 | bytes 1048576 | tf_op jit(solution)/shard_map/attn_backward_last/pallas_call | solution.py:829
  336.4 0.8 constant_dynamic-slice_fusion
  337.7 1.0 slice.52
  339.7 0.8 slice.51
  340.5 0.8 slice.55
  341.4 0.9 slice_bitcast_fusion.2
  342.3 0.8 copy.33
  343.2 1.1 copy.34
  (53 shorter events, 7.2 us)
Async XLA Ops:
  7.2 6.0 %copy-start.9 = (s32[1,320]{1,0:T(1,128)S(1)}, s32[1,320]{1,0:T(1,128)}, u32[]{:S(2)}) copy-start(s32[1,320]{1,0:T(1,128)} %param.14) | copy-start | bytes 3844
  7.2 6.4 %copy-start.4 = (bf16[1,320,960]{2,1,0:T(8,128)(2,1)S(1)}, bf16[1,320,960]{2,1,0:T(8,128)(2,1)}, u32[]{:S(2)}) copy-start(bf16[1,320,960]{2,1,0:T(8,128)(2,1)} %param.24) | copy-start | bytes 1843204
  7.2 112.6 %all-gather.3.cloned.1.call-start = ((), (), s32[]{:S(2)}) async-start(), calls=%async_computation | async-start | bytes 4423680 | tf_op jit(solution)/shard_map/all_gather | solution.py:882
  9.4 5.1 %copy-start.6 = (bf16[1,320,960]{2,1,0:T(8,128)(2,1)S(1)}, bf16[1,320,960]{2,1,0:T(8,128)(2,1)}, u32[]{:S(2)}) copy-start(bf16[1,320,960]{2,1,0:T(8,128)(2,1)} %param.13) | copy-start | bytes 1843204
  10.2 14.5 %collective-permute-start = (bf16[384,640]{1,0:T(8,128)(2,1)}, bf16[384,640]{1,0:T(8,128)(2,1)}, u32[]{:S(2)}, u32[]{:S(2)}) collective-permute-start(bf16[384,640]{1,0:T(8,128)(2,1)} %pad_maximum_fusion.3), channel_id=1, source_target_pairs={{0,16},{8,24},{16,0},{24,8},{1,17},{9,25},{17,1},{25,9},{2,18},{10... | collective-permute-start | bytes 1474568 | tf_op jit(solution)/shard_map/ppermute | solution.py:872
  14.5 1.2 copy-start.10
  14.5 1.2 copy-start.11
  14.5 2.5 copy-start.2
  14.5 2.5 copy-start.3
  336.4 3.3 copy-start.8
  337.7 2.8 copy-start.7
  339.0 2.4 copy-start.1
  340.5 1.8 copy-start.5
  341.4 1.8 copy-start
Sparse Core Ops, SparseCore 0:
  24.8 71.6 all-gather.2
